TPU v7x, 256 devices: a whole 4x4x8 slice. The times are simulated.
256 devices in a mesh: lyr: 4 (over z_lo, core), strip: 64 (over z_hi, x, y).
Axes of the slice: x: 4, y: 4, z: 8 (z_hi: 4, z_lo: 2; z = z_hi * 2 + z_lo), core: 2. Of those that a mesh axis runs over, the one named last changes fastest.
Arguments:
- nodes: bfloat16 [4, 2, 64, 512, 512], P('lyr', None, None, 'strip'), may hold values from -6 to 6
- upstream: bfloat16 [4, 2, 64, 512, 512], P('lyr', None, None, 'strip'), may hold values from -6 to 6
- usage: int32 [4, 2, 512, 512], P('lyr', None, 'strip'), may hold values from 0 to 15
- blockage: int32 [4, 2, 2, 512, 512], P('lyr', None, None, 'strip'), may hold values 0 or 1
- capacity: int32 [4, 2, 2, 512, 512], P('lyr', None, None, 'strip'), may hold values from 1 to 8
- w_src: bfloat16 [2, 128, 64], replicated, may hold values from -0.75 to 0.75
- w_dst: bfloat16 [2, 128, 64], replicated, may hold values from -0.75 to 0.75
- w_out: bfloat16 [2, 64, 128], replicated, may hold values from -0.5 to 0.5
Outputs:
- grad_nodes: bfloat16 [4, 2, 64, 512, 512], P('lyr', None, None, 'strip')
- grad_src: float32 [2, 128, 64], replicated
- grad_dst: float32 [2, 128, 64], replicated
- grad_out: float32 [2, 64, 128], replicated
All inputs are finite; a program needn't handle non-finite values. No bound on the sum of `blockage` on one device may be relied on, other than what follows from the above.
Results may differ from a plain program's by a relative error of at most 0.0058.
Values may be sent and summed in bfloat16 or wider, within the bound.
No kernel may reach another device: no remote copies, remote signals or barrier semaphores. Data moves between devices by JAX's collectives and lax.ppermute only.
A program may use at most 128 MiB of HBM per device.

v0:
```python
import math

import jax
import jax.numpy as jnp
from jax import lax
from jax.experimental import pallas as pl
from jax.experimental.pallas import tpu as pltpu
from jax.sharding import Mesh, PartitionSpec as P


F32 = jnp.float32
BF16 = jnp.bfloat16
VMEM = pltpu.VMEM
VMEM_SPEC = pl.BlockSpec(memory_space=pltpu.VMEM)
PARAMS = pltpu.CompilerParams(vmem_limit_bytes=56 * 1024 * 1024)


def mm(a, b):
    return jnp.dot(a, b, preferred_element_type=F32)


def mm_nt(a, b):
    return lax.dot_general(a, b, (((1,), (1,)), ((), ())), preferred_element_type=F32)


def load_weights(w_src_ref, w_dst_ref, w_out_ref, t):
    w_cat_t = jnp.concatenate((w_src_ref[t].astype(F32), w_dst_ref[t].astype(F32)), 0)
    w_out_t = w_out_ref[t].astype(F32).T
    return w_cat_t.T.astype(BF16), w_cat_t.astype(BF16), w_out_t.astype(BF16)


def place():
    return lax.axis_index("l"), lax.axis_index("z"), lax.axis_index("xy")


def edges(weights, x_uv, diff, gate):
    w_cat, w_cat_t, w_out_t = weights
    pre = mm(w_cat, x_uv)
    sigma = 0.5 * jnp.tanh(0.5 * pre) + 0.5
    act = pre * sigma
    slope = sigma + act * (1.0 - sigma)
    g_msg = (gate * diff).astype(BF16)
    g_pre = (mm(w_out_t, g_msg) * slope).astype(BF16)
    g_w = mm_nt(x_uv, g_pre)
    g_o = mm_nt(g_msg, act.astype(BF16))
    g_x = mm(w_cat_t, g_pre)
    return g_x, g_w, g_o


def gate_of(blockage, capacity):
    return (1 - blockage).astype(F32) * capacity.astype(F32) * 0.25


def prepare_kernel(nodes_ref, upstream_ref, usage_ref, block_ref, cap_ref,
                   xd_ref, v0_ref, v1_ref, v2_ref, v3_ref, s_ref, rim_ref,
                   xs, ds, gs):
    pair, z, xy = place()
    feat, rows, cols = nodes_ref.shape[2:]
    zs = len((v0_ref, v1_ref, v2_ref, v3_ref))
    wide = cols // zs
    for j in range(2):
        damp = lax.rsqrt(1.0 + usage_ref[0, j].astype(F32))[None]
        scaled = (nodes_ref[0, j].astype(F32) * damp).reshape(feat * rows, cols)
        given = upstream_ref[0, j].astype(F32).reshape(feat * rows, cols)
        for q in range(zs):
            xs[q] = scaled[:, q * wide:(q + 1) * wide]
            ds[q] = given[:, q * wide:(q + 1) * wide]

        def row_of(r):
            at = pl.ds(r, feat, stride=rows)
            return jnp.concatenate(
                [jnp.concatenate((xs[q, at, :], ds[q, at, :]), 0) for q in range(zs)], 1
            )

        if j == 0:
            @pl.loop(0, rows)
            def _(r):
                xd_ref[0, r] = row_of(r).astype(BF16)
                for d, v_ref in enumerate((v0_ref, v1_ref, v2_ref, v3_ref)):
                    at = pl.multiple_of(lax.rem(z + d, zs) * wide, wide)
                    v_ref[r] = xd_ref[0, r, :, pl.ds(at, wide)]
        else:
            @pl.loop(0, rows // 2)
            def _(half):
                pieces = []
                for k in range(2):
                    r = half * 2 + k
                    full = row_of(r)
                    xd_ref[1, r] = full.astype(BF16)
                    pieces.append([
                        full[:, q * wide:(q + 1) * wide].T.reshape(wide // 8, 8, 2 * feat)
                        for q in range(zs)
                    ])
                for q in range(zs):
                    both = jnp.concatenate((pieces[0][q], pieces[1][q]), 1)
                    at = pl.multiple_of(q * 8 * rows + half * 16, 16)
                    s_ref[:, pl.ds(at, 16), :] = both.astype(BF16)
    present = (pair < 3).astype(F32)
    gs[...] = jnp.zeros_like(gs)
    gs[pl.ds(pl.multiple_of(xy * 8, 8), 8), :] = gate_of(block_ref[0, 1, 1], cap_ref[0, 1, 1]) * present
    turned = [
        gs[:, q * wide:(q + 1) * wide].T.reshape(wide // 8, 8, wide) for q in range(zs)
    ]
    for q in range(0, zs, 2):
        both = jnp.concatenate((turned[q], turned[q + 1]), 1)
        s_ref[:, 8 * rows * zs + q * 8:8 * rows * zs + q * 8 + 16, :] = both.astype(BF16)
    rim_ref[...] = xd_ref[lax.rem(pair, 2), 0]


def inside_kernel(xd_ref, rim_ref, block_ref, cap_ref, w_src_ref, w_dst_ref, w_out_ref,
                  ns_ref, back_ref, g_w_ref, g_o_ref, gates, carry):
    pair, z, xy = place()
    feat = xd_ref.shape[2] // 2
    rows, cols = xd_ref.shape[1], xd_ref.shape[3]
    row_layer = lax.rem(pair, 2)
    col_layer = 1 - row_layer
    planar = load_weights(w_src_ref, w_dst_ref, w_out_ref, 0)
    via = load_weights(w_src_ref, w_dst_ref, w_out_ref, 1)
    last = lax.broadcasted_iota(jnp.int32, (rows, cols), 1) < cols - 1
    row_ids = (z * 16 + xy) * rows + lax.broadcasted_iota(jnp.int32, (rows, cols), 0)
    gates[0] = jnp.where(last, gate_of(block_ref[0, col_layer, 0], cap_ref[0, col_layer, 0]), 0.0)
    gates[1] = gate_of(block_ref[0, 0, 1], cap_ref[0, 0, 1])
    gates[2] = jnp.where(
        row_ids < cols - 1, gate_of(block_ref[0, row_layer, 0], cap_ref[0, row_layer, 0]), 0.0
    )
    g_w_ref[...] = jnp.zeros_like(g_w_ref)
    g_o_ref[...] = jnp.zeros_like(g_o_ref)
    carry[...] = jnp.zeros_like(carry)

    @pl.loop(0, rows)
    def _(r):
        low, high = xd_ref[0, r], xd_ref[1, r]
        x_uv = jnp.concatenate((low[:feat], high[:feat]), 0)
        diff = high[feat:].astype(F32) - low[feat:].astype(F32)
        g_x, g_w, g_o = edges(via, x_uv, diff, gates[1, pl.ds(r, 1), :])
        g_w_ref[1] += g_w
        g_o_ref[1] += g_o
        ns_ref[0, r] = g_x[:feat]
        ns_ref[1, r] = g_x[feat:]
        own = xd_ref[col_layer, r].astype(F32)
        side = pltpu.roll(own, cols - 1, 1)
        x_uv = jnp.concatenate((own[:feat], side[:feat]), 0).astype(BF16)
        g_x, g_w, g_o = edges(planar, x_uv, side[feat:] - own[feat:], gates[0, pl.ds(r, 1), :])
        g_w_ref[0] += g_w
        g_o_ref[0] += g_o
        ns_ref[col_layer, r] += g_x[:feat] + pltpu.roll(g_x[feat:], 1, 1)
        low = xd_ref[row_layer, r]
        high = jnp.where(r == rows - 1, rim_ref[...], xd_ref[row_layer, jnp.minimum(r + 1, rows - 1)])
        x_uv = jnp.concatenate((low[:feat], high[:feat]), 0)
        diff = high[feat:].astype(F32) - low[feat:].astype(F32)
        g_x, g_w, g_o = edges(planar, x_uv, diff, gates[2, pl.ds(r, 1), :])
        g_w_ref[0] += g_w
        g_o_ref[0] += g_o
        ns_ref[row_layer, r] += carry[...] + g_x[:feat]
        carry[...] = g_x[feat:]

    back_ref[...] = carry[...].astype(BF16)


def cross_kernel(r_ref, v0_ref, v1_ref, v2_ref, v3_ref, w_src_ref, w_dst_ref, w_out_ref,
                 gw_ref, go_ref,
                 gu_ref, gv0_ref, gv1_ref, gv2_ref, gv3_ref,
                 rf, vs, gvs, gate_rows, acc_w, acc_o, total):
    _, z, _ = place()
    zs = vs.shape[0]
    feat = vs.shape[2] // 2
    via = load_weights(w_src_ref, w_dst_ref, w_out_ref, 1)
    body = rf.shape[1]
    rf[...] = r_ref[:, :body, :].astype(F32)
    gate_rows[...] = jnp.sum(r_ref[:, body:, :].astype(F32), axis=0)
    for d, v_ref in enumerate((v0_ref, v1_ref, v2_ref, v3_ref)):
        vs[lax.rem(z + zs - d, zs)] = v_ref[...]
    acc_w[...] = jnp.zeros_like(acc_w)
    acc_o[...] = jnp.zeros_like(acc_o)

    @pl.loop(0, 8)
    def _(i):
        z2 = i // 4
        c2 = lax.rem(i, 4)
        us, vv, gg = [], [], []
        for zp in range(2):
            for cp in range(2):
                zt = z2 * 2 + zp
                cl = c2 * 2 + cp
                u = rf[:, pl.ds(zt * 64 + cl, 8, stride=8), :].reshape(128, 128).T
                us.append(u)
                vv.append(vs[zt, cl])
                gg.append(gate_rows[pl.ds(zt * 8 + cl, 1), :])
        u = jnp.concatenate(us, 1)
        v = jnp.concatenate(vv, 1)
        gate = jnp.concatenate(gg, 1)
        x_uv = jnp.concatenate((u[:feat].astype(BF16), v[:feat]), 0)
        g_x, g_w, g_o = edges(via, x_uv, v[feat:].astype(F32) - u[feat:], gate)
        acc_w[...] += g_w
        acc_o[...] += g_o
        turned = []
        for cp in range(2):
            lo, hi = cp * 128, (2 + cp) * 128
            gvs[z2 * 2, c2 * 2 + cp] = g_x[feat:, lo:lo + 128].astype(BF16)
            gvs[z2 * 2 + 1, c2 * 2 + cp] = g_x[feat:, hi:hi + 128].astype(BF16)
            both = jnp.concatenate((g_x[:feat, lo:lo + 128], g_x[:feat, hi:hi + 128]), 0)
            turned.append(both.T.reshape(16, 8, 128))
        at = pl.multiple_of(z2 * 64 + c2 * 16, 16)
        gu_ref[:, pl.ds(at, 16), :] = jnp.concatenate(turned, 1).astype(BF16)

    for d, gv_ref in enumerate((gv0_ref, gv1_ref, gv2_ref, gv3_ref)):
        gv_ref[...] = gvs[lax.rem(z + zs - d, zs)]
    total[0:64] = gw_ref[0, :feat]
    total[64:128] = gw_ref[1, :feat] + acc_w[:feat]
    total[128:192] = gw_ref[0, feat:]
    total[192:256] = gw_ref[1, feat:] + acc_w[feat:]
    total[256:320] = go_ref[0]
    total[320:384] = go_ref[1] + acc_o[...]
    for k in range(16):
        piece = total[k * 24:k * 24 + 24]
        coarse = piece.astype(BF16).astype(F32)
        both = jnp.concatenate((coarse, piece - coarse), 0)
        gu_ref[k, 128:176, :] = both.astype(BF16)


def finish_kernel(gu_ref, gv0_ref, gv1_ref, gv2_ref, gv3_ref, ns_ref, back_ref,
                  xd_ref, usage_ref, out_ref, guf, gvs, o0, o1, damps):
    pair, z, _ = place()
    zs = gvs.shape[0]
    feat = xd_ref.shape[2] // 2
    rows = xd_ref.shape[1]
    row_layer = lax.rem(pair, 2)
    guf[...] = gu_ref[:, :128, :].astype(F32)
    for d, gv_ref in enumerate((gv0_ref, gv1_ref, gv2_ref, gv3_ref)):
        gvs[lax.rem(z + d, zs)] = gv_ref[...]
    damps[...] = lax.rsqrt(1.0 + usage_ref[0].astype(F32))
    ns_ref[row_layer, 0] += back_ref[...].astype(F32)

    @pl.loop(0, rows)
    def _(r):
        low, high = ns_ref[0, r], ns_ref[1, r]
        low = low + jnp.concatenate([gvs[q, r].astype(F32) for q in range(zs)], 1)
        parts = []
        for z2 in range(2):
            block = guf[:, pl.ds(z2 * 64 + r, 8, stride=8), :].reshape(128, 128).T
            parts += [block[:feat], block[feat:]]
        high = high + jnp.concatenate(parts, 1)
        low = xd_ref[0, r, feat:, :].astype(F32) + damps[0, pl.ds(r, 1), :] * low
        high = xd_ref[1, r, feat:, :].astype(F32) + damps[1, pl.ds(r, 1), :] * high
        spots = pl.ds(r, feat, stride=rows)
        for q in range(zs):
            o0[q, spots, :] = low[:, q * 128:(q + 1) * 128]
            o1[q, spots, :] = high[:, q * 128:(q + 1) * 128]

    for q in range(zs):
        lanes = slice(q * 128, (q + 1) * 128)
        out_ref[0, 0, :, :, lanes] = o0[q].reshape(feat, rows, 128).astype(BF16)
        out_ref[0, 1, :, :, lanes] = o1[q].reshape(feat, rows, 128).astype(BF16)


def shaped(*shape, dtype=F32):
    return jax.ShapeDtypeStruct(shape, dtype)


def all_to_all(value, axes):
    return lax.all_to_all(value, axes, 0, 0, tiled=True)


def call(kernel, out, scratch, *args):
    return pl.pallas_call(
        kernel,
        out_shape=out,
        in_specs=[VMEM_SPEC] * len(args),
        out_specs=jax.tree.map(lambda _: VMEM_SPEC, out),
        scratch_shapes=scratch,
        compiler_params=PARAMS,
    )(*args)


def on_device(nodes, upstream, usage, blockage, capacity, w_src, w_dst, w_out):
    n_l, n_z, n_xy = lax.axis_size("l"), lax.axis_size("z"), lax.axis_size("xy")
    feat, rows, cols = nodes.shape[2:]
    axes = ("l", "z", "xy")

    def ident(l, k, i):
        return (l * n_z + k) * n_xy + i

    def cross_pairs(d):
        return [
            (ident(l + 1, k, i), ident(l, (k + d) % n_z, i))
            for l in range(n_l - 1) for k in range(n_z) for i in range(n_xy)
        ]

    strips = n_z * n_xy
    up = [(l * strips + s + 1, l * strips + s) for l in range(n_l) for s in range(strips - 1)]
    down = [(b, a) for a, b in up]

    xd, v0, v1, v2, v3, sent, rim = call(
        prepare_kernel,
        (
            shaped(2, rows, 2 * feat, cols, dtype=BF16),
            *[shaped(rows, 2 * feat, cols // n_z, dtype=BF16)] * 4,
            shaped(n_xy, 288, 2 * feat, dtype=BF16),
            shaped(2 * feat, cols, dtype=BF16),
        ),
        [VMEM((n_z, feat * rows, 128), F32), VMEM((n_z, feat * rows, 128), F32), VMEM((128, cols), F32)],
        nodes, upstream, usage, blockage, capacity,
    )
    rim = lax.ppermute(rim, axes, up)
    got_u = all_to_all(sent, "xy")
    got_v = [lax.ppermute(v, axes, cross_pairs(d)) for d, v in enumerate((v0, v1, v2, v3))]
    weights = (jnp.swapaxes(w_src, 1, 2), jnp.swapaxes(w_dst, 1, 2), w_out)
    ns, back, g_w, g_o = call(
        inside_kernel,
        (
            shaped(2, rows, feat, cols), shaped(feat, cols, dtype=BF16),
            shaped(2, 2 * feat, 128), shaped(2, feat, 128),
        ),
        [VMEM((3, rows, cols), F32), VMEM((feat, cols), F32)],
        xd, rim, blockage, capacity, *weights,
    )
    back = lax.ppermute(back, axes, down)
    gu, gv0, gv1, gv2, gv3 = call(
        cross_kernel,
        (
            shaped(n_xy, 176, 2 * feat, dtype=BF16),
            *[shaped(rows, feat, cols // n_z, dtype=BF16)] * 4,
        ),
        [
            VMEM((n_xy, 256, 128), F32), VMEM((n_z, rows, 2 * feat, 128), BF16),
            VMEM((n_z, rows, feat, 128), BF16), VMEM((32, 128), F32),
            VMEM((2 * feat, 128), F32), VMEM((feat, 128), F32), VMEM((384, 128), F32),
        ],
        got_u, *got_v, *weights, g_w, g_o,
    )
    got_gu = all_to_all(gu, "xy")
    got_gv = [
        lax.ppermute(g, axes, [(b, a) for a, b in cross_pairs(d)])
        for d, g in enumerate((gv0, gv1, gv2, gv3))
    ]

    scale = 1.0 / math.sqrt(2 * n_l * cols * cols)
    part = got_gu[:, 128:, :].astype(F32).reshape(n_xy, 2, 24, 128)
    part = jnp.broadcast_to(jnp.sum(part, (0, 1))[None], (16, 24, 128))
    part = all_to_all(part, ("l", "z"))
    part, got_gv[3], back = lax.optimization_barrier((part, got_gv[3], back))

    grad_nodes = call(
        finish_kernel,
        shaped(1, 2, feat, rows, cols, dtype=BF16),
        [
            VMEM((n_xy, 128, 128), F32), VMEM((n_z, rows, feat, 128), BF16),
            VMEM((n_z, feat * rows, 128), F32), VMEM((n_z, feat * rows, 128), F32),
            VMEM((2, rows, cols), F32),
        ],
        got_gu, *got_gv, ns, back, xd, usage,
    )
    part = jnp.broadcast_to(jnp.sum(part, 0)[None] * scale, (16, 24, 128))
    total = all_to_all(part, "xy").reshape(3, 2, feat, 128)
    return grad_nodes, jnp.swapaxes(total[0], 1, 2), jnp.swapaxes(total[1], 1, 2), total[2]


def solution(mesh):
    split = Mesh(mesh.devices.reshape(4, 4, 16), ("l", "z", "xy"))
    strip = ("z", "xy")
    placed = (
        P("l", None, None, strip, None),
        P("l", None, None, strip, None),
        P("l", None, strip, None),
        P("l", None, None, strip, None),
        P("l", None, None, strip, None),
        P(),
        P(),
        P(),
    )
    return jax.shard_map(
        on_device,
        mesh=split,
        in_specs=placed,
        out_specs=(P("l", None, None, strip, None), P(), P(), P()),
        check_vma=False,
    )
```

profile of v0, /device:TPU:34, one launch (start us, length us, event | category | flops | bytes accessed | tf_op | source)
XLA Modules:
  0.0 143.0 jit_solution(15361638275720381657)
XLA Ops:
  0.6 5.6 %shard_map.111 = (bf16[2,8,128,512]{3,2,1,0:T(8,128)(2,1)}, bf16[8,128,128]{2,1,0:T(8,128)(2,1)}, bf16[8,128,128]{2,1,0:T(8,128)(2,1)}, bf16[8,128,128]{2,1,0:T(...) custom-call(bf16[1,2,64,8,512]{4,3,2,1,0:T(8,128)(2,1)} %nodes_ref.1, ...), custom_call_target="tpu_custom_call" | custom-call | tf_op jit(solution)/shard_map/pallas_call | solution.py:265
  6.3 7.6 %all-to-all-start = ((bf16[16,288,128]{2,1,0:T(8,128)(2,1)}), bf16[16,288,128]{2,1,0:T(8,128)(2,1)S(1)}, u32[]{:S(2)}, u32[]{:S(2)}) async-start(bf16[16,288,128]{2,1,0:T(8,128)(2,1)} %get-tuple-element.23), calls=%async_computation | async-start | bytes 2359296 | tf_op jit(solution)/shard_map/all_to_all | solution.py:261
  13.9 1.9 %collective-permute-start = (bf16[8,128,128]{2,1,0:T(8,128)(2,1)S(1)}, bf16[8,128,128]{2,1,0:T(8,128)(2,1)S(1)}, u32[]{:S(2)}, u32[]{:S(2)}) collective-permute-start(bf16[8,128,128]{2,1,0:T(8,128)(2,1)S(1)} %copy-done.15), channel_id=1, source_target_pairs={{64,0},{65,1},{66,2},{67,3},{68,4},{69,5},{70,6},{71,7},{72,8},{73... | collective-permute-start | bytes 786440 | tf_op jit(solution)/shard_map/ppermute | solution.py:306
  15.9 3.9 %collective-permute-start.1 = (bf16[8,128,128]{2,1,0:T(8,128)(2,1)S(1)}, bf16[8,128,128]{2,1,0:T(8,128)(2,1)S(1)}, u32[]{:S(2)}, u32[]{:S(2)}) collective-permute-start(bf16[8,128,128]{2,1,0:T(8,128)(2,1)S(1)} %copy-done.14), channel_id=1, source_target_pairs={{64,16},{65,17},{66,18},{67,19},{68,20},{69,21},{70,22},{71,23},{7... | collective-permute-start | bytes 786440 | tf_op jit(solution)/shard_map/ppermute | solution.py:306
  19.8 6.3 %collective-permute-start.2 = (bf16[8,128,128]{2,1,0:T(8,128)(2,1)S(1)}, bf16[8,128,128]{2,1,0:T(8,128)(2,1)S(1)}, u32[]{:S(2)}, u32[]{:S(2)}) collective-permute-start(bf16[8,128,128]{2,1,0:T(8,128)(2,1)S(1)} %copy-done.13), channel_id=1, source_target_pairs={{64,32},{65,33},{66,34},{67,35},{68,36},{69,37},{70,38},{71,39},{7... | collective-permute-start | bytes 786440 | tf_op jit(solution)/shard_map/ppermute | solution.py:306
  26.1 1.9 %collective-permute-start.3 = (bf16[8,128,128]{2,1,0:T(8,128)(2,1)S(1)}, bf16[8,128,128]{2,1,0:T(8,128)(2,1)S(1)}, u32[]{:S(2)}, u32[]{:S(2)}) collective-permute-start(bf16[8,128,128]{2,1,0:T(8,128)(2,1)S(1)} %copy-done.12), channel_id=1, source_target_pairs={{64,48},{65,49},{66,50},{67,51},{68,52},{69,53},{70,54},{71,55},{7... | collective-permute-start | bytes 786440 | tf_op jit(solution)/shard_map/ppermute | solution.py:306
  28.1 4.6 %collective-permute-start.4 = (bf16[128,512]{1,0:T(8,128)(2,1)S(1)}, bf16[128,512]{1,0:T(8,128)(2,1)S(1)}, u32[]{:S(2)}, u32[]{:S(2)}) collective-permute-start(bf16[128,512]{1,0:T(8,128)(2,1)S(1)} %copy-done.20), channel_id=1, source_target_pairs={{1,0},{2,1},{3,2},{4,3},{5,4},{6,5},{7,6},{8,7},{9,8},{10,9},{11,1... | collective-permute-start | bytes 393224 | tf_op jit(solution)/shard_map/ppermute | solution.py:304
  32.7 2.5 %collective-permute-done.4.rim_ref = bf16[128,512]{1,0:T(8,128)(2,1)S(1)} collective-permute-done((bf16[128,512]{1,0:T(8,128)(2,1)S(1)}, bf16[128,512]{1,0:T(8,128)(2,1)S(1)}, u32[]{:S(2)}, u32[]{:S(2)}) %collective-permute-start.4) | collective-permute-done | bytes 131104 | tf_op jit(solution)/shard_map/ppermute | solution.py:304
  35.8 11.4 %shard_map.112 = (f32[2,8,64,512]{3,2,1,0:T(8,128)}, bf16[64,512]{1,0:T(8,128)(2,1)}, f32[2,128,128]{2,1,0:T(8,128)}, f32[2,64,128]{2,1,0:T(8,128)}) custom-call(bf16[2,8,128,512]{3,2,1,0:T(8,128)(2,1)} %get-tuple-element.28.xd_ref, bf16[128,512]{1,0:T(8,128)(2,1)} %copy-done.10, s32[1,2,2,8,512]{4,3,2,1,0:T(8,128)} %block_ref.3, ...), custom_call_target="tpu_custom_call" | custom-call | tf_op jit(solution)/shard_map/pallas_call | solution.py:265
  48.6 7.8 %shard_map.113 = (bf16[16,176,128]{2,1,0:T(8,128)(2,1)}, bf16[8,64,128]{2,1,0:T(8,128)(2,1)}, bf16[8,64,128]{2,1,0:T(8,128)(2,1)}, bf16[8,64,128]{2,1,0:T(8,128)(2,1)}, bf16[8,64,128]{2,1,0:T(8,128)(2,1)}) custom-call(bf16[16,288,128]{2,1,0:T(8,128)(2,1)} %copy-done, bf16[8,128,128]{2,1,0:T(8,128)(2,1)} %copy-done.2, bf16[8,128,128]{2,1,0:T(8,128)(2,1)} %copy-done.3, ...), custom_call_target="tpu_custom_call" | custom-call | tf_op jit(solution)/shard_map/pallas_call | solution.py:265
  56.4 31.3 %all_to_all.20.gu_ref = bf16[16,176,128]{2,1,0:T(8,128)(2,1)S(1)} all-to-all(bf16[16,176,128]{2,1,0:T(8,128)(2,1)} %get-tuple-element.32), channel_id=1, replica_groups=mesh['l'=4,'z'=4,'xy'=16] {'xy'}, dimensions={0} | all-to-all | bytes 1441792 | tf_op jit(solution)/shard_map/all_to_all | solution.py:261
  87.8 0.8 broadcast_in_dim.4
  88.6 6.1 %all-to-all-start.2 = ((f32[16,24,128]{2,1,0:T(8,128)}), f32[16,24,128]{2,1,0:T(8,128)S(1)}, u32[]{:S(2)}, u32[]{:S(2)}) async-start(f32[16,24,128]{2,1,0:T(8,128)} %broadcast_in_dim.4), calls=%async_computation.2 | async-start | bytes 393216 | tf_op jit(solution)/shard_map/all_to_all | solution.py:261
  94.7 4.0 %collective-permute-start.8 = (bf16[8,64,128]{2,1,0:T(8,128)(2,1)S(1)}, bf16[8,64,128]{2,1,0:T(8,128)(2,1)S(1)}, u32[]{:S(2)}, u32[]{:S(2)}) collective-permute-start(bf16[8,64,128]{2,1,0:T(8,128)(2,1)S(1)} %copy-done.19), channel_id=1, source_target_pairs={{48,64},{49,65},{50,66},{51,67},{52,68},{53,69},{54,70},{55,71},{5... | collective-permute-start | bytes 393224 | tf_op jit(solution)/shard_map/ppermute | solution.py:333
  98.7 2.2 %collective-permute-start.9 = (bf16[64,512]{1,0:T(8,128)(2,1)S(1)}, bf16[64,512]{1,0:T(8,128)(2,1)S(1)}, u32[]{:S(2)}, u32[]{:S(2)}) collective-permute-start(bf16[64,512]{1,0:T(8,128)(2,1)S(1)} %copy-done.21), channel_id=1, source_target_pairs={{0,1},{1,2},{2,3},{3,4},{4,5},{5,6},{6,7},{7,8},{8,9},{9,10},{10,1... | collective-permute-start | bytes 196616 | tf_op jit(solution)/shard_map/ppermute | solution.py:317
  100.8 6.1 %collective-permute-done.9.back_ref = bf16[64,512]{1,0:T(8,128)(2,1)S(1)} collective-permute-done((bf16[64,512]{1,0:T(8,128)(2,1)S(1)}, bf16[64,512]{1,0:T(8,128)(2,1)S(1)}, u32[]{:S(2)}, u32[]{:S(2)}) %collective-permute-start.9) | collective-permute-done | bytes 65568 | tf_op jit(solution)/shard_map/ppermute | solution.py:317
  107.0 1.5 %collective-permute-done.8.gv3_ref = bf16[8,64,128]{2,1,0:T(8,128)(2,1)S(1)} collective-permute-done((bf16[8,64,128]{2,1,0:T(8,128)(2,1)S(1)}, bf16[8,64,128]{2,1,0:T(8,128)(2,1)S(1)}, u32[]{:S(2)}, u32[]{:S(2)}) %collective-permute-start.8) | collective-permute-done | bytes 131104 | tf_op jit(solution)/shard_map/ppermute | solution.py:333
  109.2 5.9 %all-to-all-start.3 = ((f32[16,24,128]{2,1,0:T(8,128)}), f32[16,24,128]{2,1,0:T(8,128)S(1)}, u32[]{:S(2)}, u32[]{:S(2)}) async-start(f32[16,24,128]{2,1,0:T(8,128)} %broadcast_in_dim.5), calls=%async_computation.3 | async-start | bytes 393216 | tf_op jit(solution)/shard_map/all_to_all | solution.py:261
  115.0 1.9 %collective-permute-start.5 = (bf16[8,64,128]{2,1,0:T(8,128)(2,1)S(1)}, bf16[8,64,128]{2,1,0:T(8,128)(2,1)S(1)}, u32[]{:S(2)}, u32[]{:S(2)}) collective-permute-start(bf16[8,64,128]{2,1,0:T(8,128)(2,1)S(1)} %copy-done.18), channel_id=1, source_target_pairs={{0,64},{1,65},{2,66},{3,67},{4,68},{5,69},{6,70},{7,71},{8,72},{9,... | collective-permute-start | bytes 393224 | tf_op jit(solution)/shard_map/ppermute | solution.py:333
  117.0 1.9 %collective-permute-start.6 = (bf16[8,64,128]{2,1,0:T(8,128)(2,1)S(1)}, bf16[8,64,128]{2,1,0:T(8,128)(2,1)S(1)}, u32[]{:S(2)}, u32[]{:S(2)}) collective-permute-start(bf16[8,64,128]{2,1,0:T(8,128)(2,1)S(1)} %copy-done.17), channel_id=1, source_target_pairs={{16,64},{17,65},{18,66},{19,67},{20,68},{21,69},{22,70},{23,71},{2... | collective-permute-start | bytes 393224 | tf_op jit(solution)/shard_map/ppermute | solution.py:333
  118.9 2.8 %collective-permute-start.7 = (bf16[8,64,128]{2,1,0:T(8,128)(2,1)S(1)}, bf16[8,64,128]{2,1,0:T(8,128)(2,1)S(1)}, u32[]{:S(2)}, u32[]{:S(2)}) collective-permute-start(bf16[8,64,128]{2,1,0:T(8,128)(2,1)S(1)} %copy-done.16), channel_id=1, source_target_pairs={{32,64},{33,65},{34,66},{35,67},{36,68},{37,69},{38,70},{39,71},{4... | collective-permute-start | bytes 393224 | tf_op jit(solution)/shard_map/ppermute | solution.py:333
  121.8 7.7 %collective-permute-done.6.gv1_ref = bf16[8,64,128]{2,1,0:T(8,128)(2,1)S(1)} collective-permute-done((bf16[8,64,128]{2,1,0:T(8,128)(2,1)S(1)}, bf16[8,64,128]{2,1,0:T(8,128)(2,1)S(1)}, u32[]{:S(2)}, u32[]{:S(2)}) %collective-permute-start.6) | collective-permute-done | bytes 131104 | tf_op jit(solution)/shard_map/ppermute | solution.py:333
  129.4 7.4 %collective-permute-done.7.gv2_ref = bf16[8,64,128]{2,1,0:T(8,128)(2,1)S(1)} collective-permute-done((bf16[8,64,128]{2,1,0:T(8,128)(2,1)S(1)}, bf16[8,64,128]{2,1,0:T(8,128)(2,1)S(1)}, u32[]{:S(2)}, u32[]{:S(2)}) %collective-permute-start.7) | collective-permute-done | bytes 131104 | tf_op jit(solution)/shard_map/ppermute | solution.py:333
  137.5 4.8 %shard_map.114 = bf16[1,2,64,8,512]{4,3,2,1,0:T(8,128)(2,1)} custom-call(bf16[16,176,128]{2,1,0:T(8,128)(2,1)} %copy-done.1, bf16[8,64,128]{2,1,0:T(8,128)(2,1)} %copy-done.7, bf16[8,64,128]{2,1,0:T(8,128)(2,1)} %copy-done.8, bf16[8,64,128]{2,1,0:T(8,128)(2,1)} %copy-done.9, bf16[8,64,128]{2,1,0:T(8,128)(2,1)} %copy-done.6, ...), custom_call_target="tpu_custom_call" | custom-call | tf_op jit(solution)/shard_map/pallas_call | solution.py:265
  (58 shorter events, 4.1 us)
Async XLA Ops:
  6.3 19.8 %copy-start.12 = (bf16[8,128,128]{2,1,0:T(8,128)(2,1)S(1)}, bf16[8,128,128]{2,1,0:T(8,128)(2,1)}, u32[]{:S(2)}) copy-start(bf16[8,128,128]{2,1,0:T(8,128)(2,1)} %get-tuple-element.27) | copy-start | bytes 786436
  6.3 21.8 %copy-start.20 = (bf16[128,512]{1,0:T(8,128)(2,1)S(1)}, bf16[128,512]{1,0:T(8,128)(2,1)}, u32[]{:S(2)}) copy-start(bf16[128,512]{1,0:T(8,128)(2,1)} %get-tuple-element.29) | copy-start | bytes 393220
  6.3 41.0 %all-to-all-start = ((bf16[16,288,128]{2,1,0:T(8,128)(2,1)}), bf16[16,288,128]{2,1,0:T(8,128)(2,1)S(1)}, u32[]{:S(2)}, u32[]{:S(2)}) async-start(bf16[16,288,128]{2,1,0:T(8,128)(2,1)} %get-tuple-element.23), calls=%async_computation | async-start | bytes 2359296 | tf_op jit(solution)/shard_map/all_to_all | solution.py:261
  13.9 33.3 %collective-permute-start = (bf16[8,128,128]{2,1,0:T(8,128)(2,1)S(1)}, bf16[8,128,128]{2,1,0:T(8,128)(2,1)S(1)}, u32[]{:S(2)}, u32[]{:S(2)}) collective-permute-start(bf16[8,128,128]{2,1,0:T(8,128)(2,1)S(1)} %copy-done.15), channel_id=1, source_target_pairs={{64,0},{65,1},{66,2},{67,3},{68,4},{69,5},{70,6},{71,7},{72,8},{73... | collective-permute-start | bytes 786440 | tf_op jit(solution)/shard_map/ppermute | solution.py:306
  15.9 31.4 %collective-permute-start.1 = (bf16[8,128,128]{2,1,0:T(8,128)(2,1)S(1)}, bf16[8,128,128]{2,1,0:T(8,128)(2,1)S(1)}, u32[]{:S(2)}, u32[]{:S(2)}) collective-permute-start(bf16[8,128,128]{2,1,0:T(8,128)(2,1)S(1)} %copy-done.14), channel_id=1, source_target_pairs={{64,16},{65,17},{66,18},{67,19},{68,20},{69,21},{70,22},{71,23},{7... | collective-permute-start | bytes 786440 | tf_op jit(solution)/shard_map/ppermute | solution.py:306
  19.8 27.5 %collective-permute-start.2 = (bf16[8,128,128]{2,1,0:T(8,128)(2,1)S(1)}, bf16[8,128,128]{2,1,0:T(8,128)(2,1)S(1)}, u32[]{:S(2)}, u32[]{:S(2)}) collective-permute-start(bf16[8,128,128]{2,1,0:T(8,128)(2,1)S(1)} %copy-done.13), channel_id=1, source_target_pairs={{64,32},{65,33},{66,34},{67,35},{68,36},{69,37},{70,38},{71,39},{7... | collective-permute-start | bytes 786440 | tf_op jit(solution)/shard_map/ppermute | solution.py:306
  26.1 21.2 %collective-permute-start.3 = (bf16[8,128,128]{2,1,0:T(8,128)(2,1)S(1)}, bf16[8,128,128]{2,1,0:T(8,128)(2,1)S(1)}, u32[]{:S(2)}, u32[]{:S(2)}) collective-permute-start(bf16[8,128,128]{2,1,0:T(8,128)(2,1)S(1)} %copy-done.12), channel_id=1, source_target_pairs={{64,48},{65,49},{66,50},{67,51},{68,52},{69,53},{70,54},{71,55},{7... | collective-permute-start | bytes 786440 | tf_op jit(solution)/shard_map/ppermute | solution.py:306
  28.1 7.1 %collective-permute-start.4 = (bf16[128,512]{1,0:T(8,128)(2,1)S(1)}, bf16[128,512]{1,0:T(8,128)(2,1)S(1)}, u32[]{:S(2)}, u32[]{:S(2)}) collective-permute-start(bf16[128,512]{1,0:T(8,128)(2,1)S(1)} %copy-done.20), channel_id=1, source_target_pairs={{1,0},{2,1},{3,2},{4,3},{5,4},{6,5},{7,6},{8,7},{9,8},{10,9},{11,1... | collective-permute-start | bytes 393224 | tf_op jit(solution)/shard_map/ppermute | solution.py:304
  48.6 50.0 %copy-start.21 = (bf16[64,512]{1,0:T(8,128)(2,1)S(1)}, bf16[64,512]{1,0:T(8,128)(2,1)}, u32[]{:S(2)}) copy-start(bf16[64,512]{1,0:T(8,128)(2,1)} %get-tuple-element.37) | copy-start | bytes 196612
  56.4 38.3 %copy-start.19 = (bf16[8,64,128]{2,1,0:T(8,128)(2,1)S(1)}, bf16[8,64,128]{2,1,0:T(8,128)(2,1)}, u32[]{:S(2)}) copy-start(bf16[8,64,128]{2,1,0:T(8,128)(2,1)} %get-tuple-element.36) | copy-start | bytes 393220
  56.4 58.6 %copy-start.18 = (bf16[8,64,128]{2,1,0:T(8,128)(2,1)S(1)}, bf16[8,64,128]{2,1,0:T(8,128)(2,1)}, u32[]{:S(2)}) copy-start(bf16[8,64,128]{2,1,0:T(8,128)(2,1)} %get-tuple-element.33) | copy-start | bytes 393220
  56.4 60.5 %copy-start.17 = (bf16[8,64,128]{2,1,0:T(8,128)(2,1)S(1)}, bf16[8,64,128]{2,1,0:T(8,128)(2,1)}, u32[]{:S(2)}) copy-start(bf16[8,64,128]{2,1,0:T(8,128)(2,1)} %get-tuple-element.34) | copy-start | bytes 393220
  56.4 62.5 %copy-start.16 = (bf16[8,64,128]{2,1,0:T(8,128)(2,1)S(1)}, bf16[8,64,128]{2,1,0:T(8,128)(2,1)}, u32[]{:S(2)}) copy-start(bf16[8,64,128]{2,1,0:T(8,128)(2,1)} %get-tuple-element.35) | copy-start | bytes 393220
  87.8 49.1 %copy-start.1 = (bf16[16,176,128]{2,1,0:T(8,128)(2,1)}, bf16[16,176,128]{2,1,0:T(8,128)(2,1)S(1)}, u32[]{:S(2)}) copy-start(bf16[16,176,128]{2,1,0:T(8,128)(2,1)S(1)} %all_to_all.20.gu_ref) | copy-start | bytes 2162692
  88.6 19.8 %all-to-all-start.2 = ((f32[16,24,128]{2,1,0:T(8,128)}), f32[16,24,128]{2,1,0:T(8,128)S(1)}, u32[]{:S(2)}, u32[]{:S(2)}) async-start(f32[16,24,128]{2,1,0:T(8,128)} %broadcast_in_dim.4), calls=%async_computation.2 | async-start | bytes 393216 | tf_op jit(solution)/shard_map/all_to_all | solution.py:261
  94.7 13.7 %collective-permute-start.8 = (bf16[8,64,128]{2,1,0:T(8,128)(2,1)S(1)}, bf16[8,64,128]{2,1,0:T(8,128)(2,1)S(1)}, u32[]{:S(2)}, u32[]{:S(2)}) collective-permute-start(bf16[8,64,128]{2,1,0:T(8,128)(2,1)S(1)} %copy-done.19), channel_id=1, source_target_pairs={{48,64},{49,65},{50,66},{51,67},{52,68},{53,69},{54,70},{55,71},{5... | collective-permute-start | bytes 393224 | tf_op jit(solution)/shard_map/ppermute | solution.py:333
  98.7 8.3 %collective-permute-start.9 = (bf16[64,512]{1,0:T(8,128)(2,1)S(1)}, bf16[64,512]{1,0:T(8,128)(2,1)S(1)}, u32[]{:S(2)}, u32[]{:S(2)}) collective-permute-start(bf16[64,512]{1,0:T(8,128)(2,1)S(1)} %copy-done.21), channel_id=1, source_target_pairs={{0,1},{1,2},{2,3},{3,4},{4,5},{5,6},{6,7},{7,8},{8,9},{9,10},{10,1... | collective-permute-start | bytes 196616 | tf_op jit(solution)/shard_map/ppermute | solution.py:317
  106.9 29.9 %copy-start.11 = (bf16[64,512]{1,0:T(8,128)(2,1)}, bf16[64,512]{1,0:T(8,128)(2,1)S(1)}, u32[]{:S(2)}) copy-start(bf16[64,512]{1,0:T(8,128)(2,1)S(1)} %collective-permute-done.9.back_ref) | copy-start | bytes 196612
  108.4 28.5 %copy-start.6 = (bf16[8,64,128]{2,1,0:T(8,128)(2,1)}, bf16[8,64,128]{2,1,0:T(8,128)(2,1)S(1)}, u32[]{:S(2)}) copy-start(bf16[8,64,128]{2,1,0:T(8,128)(2,1)S(1)} %collective-permute-done.8.gv3_ref) | copy-start | bytes 393220
  109.2 33.2 %all-to-all-start.3 = ((f32[16,24,128]{2,1,0:T(8,128)}), f32[16,24,128]{2,1,0:T(8,128)S(1)}, u32[]{:S(2)}, u32[]{:S(2)}) async-start(f32[16,24,128]{2,1,0:T(8,128)} %broadcast_in_dim.5), calls=%async_computation.3 | async-start | bytes 393216 | tf_op jit(solution)/shard_map/all_to_all | solution.py:261
  115.0 6.7 %collective-permute-start.5 = (bf16[8,64,128]{2,1,0:T(8,128)(2,1)S(1)}, bf16[8,64,128]{2,1,0:T(8,128)(2,1)S(1)}, u32[]{:S(2)}, u32[]{:S(2)}) collective-permute-start(bf16[8,64,128]{2,1,0:T(8,128)(2,1)S(1)} %copy-done.18), channel_id=1, source_target_pairs={{0,64},{1,65},{2,66},{3,67},{4,68},{5,69},{6,70},{7,71},{8,72},{9,... | collective-permute-start | bytes 393224 | tf_op jit(solution)/shard_map/ppermute | solution.py:333
  117.0 12.5 %collective-permute-start.6 = (bf16[8,64,128]{2,1,0:T(8,128)(2,1)S(1)}, bf16[8,64,128]{2,1,0:T(8,128)(2,1)S(1)}, u32[]{:S(2)}, u32[]{:S(2)}) collective-permute-start(bf16[8,64,128]{2,1,0:T(8,128)(2,1)S(1)} %copy-done.17), channel_id=1, source_target_pairs={{16,64},{17,65},{18,66},{19,67},{20,68},{21,69},{22,70},{23,71},{2... | collective-permute-start | bytes 393224 | tf_op jit(solution)/shard_map/ppermute | solution.py:333
  118.9 17.9 %collective-permute-start.7 = (bf16[8,64,128]{2,1,0:T(8,128)(2,1)S(1)}, bf16[8,64,128]{2,1,0:T(8,128)(2,1)S(1)}, u32[]{:S(2)}, u32[]{:S(2)}) collective-permute-start(bf16[8,64,128]{2,1,0:T(8,128)(2,1)S(1)} %copy-done.16), channel_id=1, source_target_pairs={{32,64},{33,65},{34,66},{35,67},{36,68},{37,69},{38,70},{39,71},{4... | collective-permute-start | bytes 393224 | tf_op jit(solution)/shard_map/ppermute | solution.py:333
  121.8 15.1 %copy-start.7 = (bf16[8,64,128]{2,1,0:T(8,128)(2,1)}, bf16[8,64,128]{2,1,0:T(8,128)(2,1)S(1)}, u32[]{:S(2)}) copy-start(bf16[8,64,128]{2,1,0:T(8,128)(2,1)S(1)} %collective-permute-done.5.gv0_ref) | copy-start | bytes 393220
  (11 other events, 44.1 us)
where the time goes:
time: 144 us; the launch traced here: 143 us
  starting transfers between devices  51 us (35%)
  blocking collectives  31.3 us (22%)
  Pallas kernels  29.7 us (21%)
  waiting for transfers between devices  25.2 us (18%)
  local copies, waits for them, and re-layouts  4.81 us (3%)
    all_to_all x1, blocking collectives, all_to_all(): return lax.all_to_all(value, axes, 0, 0, tiled=True)  31.3 us
    pallas_call x4, Pallas kernels, call(): pl.pallas_call(kernel, out_shape=out, in_specs=[VMEM_SPEC] * len(args), o...  29.7 us
    all_to_all x3, starting transfers between devices, all_to_all(): return lax.all_to_all(value, axes, 0, 0, tiled=True)  19.6 us
    ppermute x4, waiting for transfers between devices, on_device(): lax.ppermute(g, axes, [(b, a) for a, b in cross_pairs(d)])  16.6 us
    ppermute x4, starting transfers between devices, on_device(): lax.ppermute(v, axes, cross_pairs(d))  14.1 us
    ppermute x4, starting transfers between devices, on_device(): lax.ppermute(g, axes, [(b, a) for a, b in cross_pairs(d)])  10.6 us
    ppermute x1, waiting for transfers between devices, on_device(): back = lax.ppermute(back, axes, down)  6.1 us
    ppermute x1, starting transfers between devices, on_device(): rim = lax.ppermute(rim, axes, up)  4.58 us
  transfers between devices with their start and end apart: 13, of which 5 were waited for; matrix products, arithmetic and copies ran while one was open for 0% of the time, Pallas kernels for 11%

commit v1 on v0

--- a/solution.py
+++ b/solution.py
@@ -12,7 +12,21 @@
 BF16 = jnp.bfloat16
 VMEM = pltpu.VMEM
 VMEM_SPEC = pl.BlockSpec(memory_space=pltpu.VMEM)
-PARAMS = pltpu.CompilerParams(vmem_limit_bytes=56 * 1024 * 1024)
+HBM_SPEC = pl.BlockSpec(memory_space=pltpu.HBM)
+DMA = pltpu.SemaphoreType.DMA
+PARAMS = pltpu.CompilerParams(vmem_limit_bytes=24 * 1024 * 1024)
+
+
+def copies(sems, *pairs):
+    made = [pltpu.make_async_copy(a, b, sems.at[i]) for i, (a, b) in enumerate(pairs)]
+    for copy in made:
+        copy.start()
+    return made
+
+
+def finish(made):
+    for copy in made:
+        copy.wait()
 
 
 def mm(a, b):
@@ -51,17 +65,30 @@
     return (1 - blockage).astype(F32) * capacity.astype(F32) * 0.25
 
 
-def prepare_kernel(nodes_ref, upstream_ref, usage_ref, block_ref, cap_ref,
-                   xd_ref, v0_ref, v1_ref, v2_ref, v3_ref, s_ref, rim_ref,
-                   xs, ds, gs):
+def prepare_kernel(nodes_hbm, upstream_hbm, usage_hbm, block_hbm, cap_hbm,
+                   xd_hbm, v0_hbm, v1_hbm, v2_hbm, v3_hbm, s_hbm, rim_hbm,
+                   xs, ds, gs, nodes_ref, upstream_ref, usage_ref, block_ref, cap_ref,
+                   xd_ref, v_ref, s_ref, in_sems, out_sems):
     pair, z, xy = place()
-    feat, rows, cols = nodes_ref.shape[2:]
-    zs = len((v0_ref, v1_ref, v2_ref, v3_ref))
+    feat, rows, cols = nodes_ref.shape[1:]
+    zs = v_ref.shape[0]
     wide = cols // zs
+    loads = copies(
+        in_sems,
+        (usage_hbm.at[0], usage_ref),
+        (nodes_hbm.at[0, 0], nodes_ref.at[0]),
+        (upstream_hbm.at[0, 0], upstream_ref.at[0]),
+        (nodes_hbm.at[0, 1], nodes_ref.at[1]),
+        (upstream_hbm.at[0, 1], upstream_ref.at[1]),
+        (block_hbm.at[0, 1, 1], block_ref),
+        (cap_hbm.at[0, 1, 1], cap_ref),
+    )
+    stores = []
     for j in range(2):
-        damp = lax.rsqrt(1.0 + usage_ref[0, j].astype(F32))[None]
-        scaled = (nodes_ref[0, j].astype(F32) * damp).reshape(feat * rows, cols)
-        given = upstream_ref[0, j].astype(F32).reshape(feat * rows, cols)
+        finish(loads[:3] if j == 0 else loads[3:])
+        damp = lax.rsqrt(1.0 + usage_ref[j].astype(F32))[None]
+        scaled = (nodes_ref[j].astype(F32) * damp).reshape(feat * rows, cols)
+        given = upstream_ref[j].astype(F32).reshape(feat * rows, cols)
         for q in range(zs):
             xs[q] = scaled[:, q * wide:(q + 1) * wide]
             ds[q] = given[:, q * wide:(q + 1) * wide]
@@ -76,9 +103,18 @@
             @pl.loop(0, rows)
             def _(r):
                 xd_ref[0, r] = row_of(r).astype(BF16)
-                for d, v_ref in enumerate((v0_ref, v1_ref, v2_ref, v3_ref)):
+                for d in range(zs):
                     at = pl.multiple_of(lax.rem(z + d, zs) * wide, wide)
-                    v_ref[r] = xd_ref[0, r, :, pl.ds(at, wide)]
+                    v_ref[d, r] = xd_ref[0, r, :, pl.ds(at, wide)]
+
+            stores += copies(
+                out_sems,
+                (xd_ref.at[0], xd_hbm.at[0]),
+                (v_ref.at[0], v0_hbm),
+                (v_ref.at[1], v1_hbm),
+                (v_ref.at[2], v2_hbm),
+                (v_ref.at[3], v3_hbm),
+            )
         else:
             @pl.loop(0, rows // 2)
             def _(half):
@@ -97,19 +133,42 @@
                     s_ref[:, pl.ds(at, 16), :] = both.astype(BF16)
     present = (pair < 3).astype(F32)
     gs[...] = jnp.zeros_like(gs)
-    gs[pl.ds(pl.multiple_of(xy * 8, 8), 8), :] = gate_of(block_ref[0, 1, 1], cap_ref[0, 1, 1]) * present
+    gs[pl.ds(pl.multiple_of(xy * 8, 8), 8), :] = gate_of(block_ref[...], cap_ref[...]) * present
     turned = [
         gs[:, q * wide:(q + 1) * wide].T.reshape(wide // 8, 8, wide) for q in range(zs)
     ]
     for q in range(0, zs, 2):
         both = jnp.concatenate((turned[q], turned[q + 1]), 1)
         s_ref[:, 8 * rows * zs + q * 8:8 * rows * zs + q * 8 + 16, :] = both.astype(BF16)
-    rim_ref[...] = xd_ref[lax.rem(pair, 2), 0]
-
-
-def inside_kernel(xd_ref, rim_ref, block_ref, cap_ref, w_src_ref, w_dst_ref, w_out_ref,
-                  ns_ref, back_ref, g_w_ref, g_o_ref, gates, carry):
+    stores += copies(
+        out_sems.at[5:],
+        (s_ref, s_hbm),
+        (xd_ref.at[lax.rem(pair, 2), 0], rim_hbm),
+        (xd_ref.at[1], xd_hbm.at[1]),
+    )
+    finish(stores)
+
+
+def inside_kernel(rim_ref, xd_hbm, block_hbm, cap_hbm, w_src_hbm, w_dst_hbm, w_out_hbm,
+                  ns_hbm, back_hbm, g_w_hbm, g_o_hbm,
+                  gates, carry, xd_ref, block_ref, cap_ref, w_src_ref, w_dst_ref, w_out_ref,
+                  ns_ref, back_ref, g_w_ref, g_o_ref, in_sems, row_sems, ns_sems, out_sems):
     pair, z, xy = place()
+    loads = copies(
+        in_sems,
+        (block_hbm, block_ref), (cap_hbm, cap_ref),
+        (w_src_hbm, w_src_ref), (w_dst_hbm, w_dst_ref), (w_out_hbm, w_out_ref),
+    )
+
+    def row_in(r):
+        return pltpu.make_async_copy(xd_hbm.at[:, r], xd_ref.at[:, r], row_sems.at[r])
+
+    def row_out(r):
+        return pltpu.make_async_copy(ns_ref.at[:, r], ns_hbm.at[:, r], ns_sems.at[r])
+
+    for r in range(xd_ref.shape[1]):
+        row_in(r).start()
+    finish(loads)
     feat = xd_ref.shape[2] // 2
     rows, cols = xd_ref.shape[1], xd_ref.shape[3]
     row_layer = lax.rem(pair, 2)
@@ -126,9 +185,14 @@
     g_w_ref[...] = jnp.zeros_like(g_w_ref)
     g_o_ref[...] = jnp.zeros_like(g_o_ref)
     carry[...] = jnp.zeros_like(carry)
-
-    @pl.loop(0, rows)
+    row_in(0).wait()
+
+    @pl.loop(0, rows, unroll=2)
     def _(r):
+        @pl.when(r + 1 < rows)
+        def _():
+            row_in(r + 1).wait()
+
         low, high = xd_ref[0, r], xd_ref[1, r]
         x_uv = jnp.concatenate((low[:feat], high[:feat]), 0)
         diff = high[feat:].astype(F32) - low[feat:].astype(F32)
@@ -153,18 +217,28 @@
         g_o_ref[0] += g_o
         ns_ref[row_layer, r] += carry[...] + g_x[:feat]
         carry[...] = g_x[feat:]
+        row_out(r).start()
 
     back_ref[...] = carry[...].astype(BF16)
-
-
-def cross_kernel(r_ref, v0_ref, v1_ref, v2_ref, v3_ref, w_src_ref, w_dst_ref, w_out_ref,
-                 gw_ref, go_ref,
-                 gu_ref, gv0_ref, gv1_ref, gv2_ref, gv3_ref,
-                 rf, vs, gvs, gate_rows, acc_w, acc_o, total):
+    stores = copies(out_sems, (back_ref, back_hbm), (g_w_ref, g_w_hbm), (g_o_ref, g_o_hbm))
+    for r in range(rows):
+        row_out(r).wait()
+    finish(stores)
+
+
+def cross_kernel(r_ref, v0_ref, v1_ref, v2_ref, v3_ref, w_src_hbm, w_dst_hbm, w_out_hbm,
+                 gw_hbm, go_hbm,
+                 gu_hbm, gv0_hbm, gv1_hbm, gv2_hbm, gv3_hbm,
+                 rf, vs, gvs, gate_rows, acc_w, acc_o, total,
+                 w_src_ref, w_dst_ref, w_out_ref, gw_ref, go_ref, gu_ref, in_sems, out_sems):
     _, z, _ = place()
+    loads = copies(
+        in_sems,
+        (w_src_hbm, w_src_ref), (w_dst_hbm, w_dst_ref), (w_out_hbm, w_out_ref),
+        (gw_hbm, gw_ref), (go_hbm, go_ref),
+    )
     zs = vs.shape[0]
     feat = vs.shape[2] // 2
-    via = load_weights(w_src_ref, w_dst_ref, w_out_ref, 1)
     body = rf.shape[1]
     rf[...] = r_ref[:, :body, :].astype(F32)
     gate_rows[...] = jnp.sum(r_ref[:, body:, :].astype(F32), axis=0)
@@ -172,8 +246,10 @@
         vs[lax.rem(z + zs - d, zs)] = v_ref[...]
     acc_w[...] = jnp.zeros_like(acc_w)
     acc_o[...] = jnp.zeros_like(acc_o)
-
-    @pl.loop(0, 8)
+    finish(loads)
+    via = load_weights(w_src_ref, w_dst_ref, w_out_ref, 1)
+
+    @pl.loop(0, 8, unroll=2)
     def _(i):
         z2 = i // 4
         c2 = lax.rem(i, 4)
@@ -203,8 +279,13 @@
         at = pl.multiple_of(z2 * 64 + c2 * 16, 16)
         gu_ref[:, pl.ds(at, 16), :] = jnp.concatenate(turned, 1).astype(BF16)
 
-    for d, gv_ref in enumerate((gv0_ref, gv1_ref, gv2_ref, gv3_ref)):
-        gv_ref[...] = gvs[lax.rem(z + zs - d, zs)]
+    stores = copies(
+        out_sems,
+        *[
+            (gvs.at[lax.rem(z + zs - d, zs)], gv_hbm)
+            for d, gv_hbm in enumerate((gv0_hbm, gv1_hbm, gv2_hbm, gv3_hbm))
+        ],
+    )
     total[0:64] = gw_ref[0, :feat]
     total[64:128] = gw_ref[1, :feat] + acc_w[:feat]
     total[128:192] = gw_ref[0, feat:]
@@ -216,11 +297,27 @@
         coarse = piece.astype(BF16).astype(F32)
         both = jnp.concatenate((coarse, piece - coarse), 0)
         gu_ref[k, 128:176, :] = both.astype(BF16)
-
-
-def finish_kernel(gu_ref, gv0_ref, gv1_ref, gv2_ref, gv3_ref, ns_ref, back_ref,
-                  xd_ref, usage_ref, out_ref, guf, gvs, o0, o1, damps):
+    stores += copies(out_sems.at[4:], (gu_ref, gu_hbm))
+    finish(stores)
+
+
+def finish_kernel(gu_ref, gv0_ref, gv1_ref, gv2_ref, gv3_ref, back_ref, ns_hbm,
+                  xd_hbm, usage_hbm, out_hbm,
+                  guf, gvs, o0, o1, damps, ns_ref, xd_ref, usage_ref, out_ref,
+                  in_sems, ns_sems, xd_sems, out_sems):
     pair, z, _ = place()
+    loads = copies(in_sems, (usage_hbm, usage_ref))
+
+    def rows_in(r):
+        return (
+            pltpu.make_async_copy(ns_hbm.at[:, r], ns_ref.at[:, r], ns_sems.at[r]),
+            pltpu.make_async_copy(xd_hbm.at[:, r], xd_ref.at[:, r], xd_sems.at[r]),
+        )
+
+    for r in range(xd_ref.shape[1]):
+        for copy in rows_in(r):
+            copy.start()
+    finish(loads)
     zs = gvs.shape[0]
     feat = xd_ref.shape[2] // 2
     rows = xd_ref.shape[1]
@@ -229,10 +326,15 @@
     for d, gv_ref in enumerate((gv0_ref, gv1_ref, gv2_ref, gv3_ref)):
         gvs[lax.rem(z + d, zs)] = gv_ref[...]
     damps[...] = lax.rsqrt(1.0 + usage_ref[0].astype(F32))
-    ns_ref[row_layer, 0] += back_ref[...].astype(F32)
-
-    @pl.loop(0, rows)
+
+    @pl.loop(0, rows, unroll=2)
     def _(r):
+        finish(rows_in(r))
+
+        @pl.when(r == 0)
+        def _():
+            ns_ref[row_layer, 0] += back_ref[...].astype(F32)
+
         low, high = ns_ref[0, r], ns_ref[1, r]
         low = low + jnp.concatenate([gvs[q, r].astype(F32) for q in range(zs)], 1)
         parts = []
@@ -247,26 +349,30 @@
             o0[q, spots, :] = low[:, q * 128:(q + 1) * 128]
             o1[q, spots, :] = high[:, q * 128:(q + 1) * 128]
 
-    for q in range(zs):
-        lanes = slice(q * 128, (q + 1) * 128)
-        out_ref[0, 0, :, :, lanes] = o0[q].reshape(feat, rows, 128).astype(BF16)
-        out_ref[0, 1, :, :, lanes] = o1[q].reshape(feat, rows, 128).astype(BF16)
+    stores = []
+    for j, done in enumerate((o0, o1)):
+        for q in range(zs):
+            lanes = slice(q * 128, (q + 1) * 128)
+            out_ref[j, :, :, lanes] = done[q].reshape(feat, rows, 128).astype(BF16)
+        stores += copies(out_sems.at[j:], (out_ref.at[j], out_hbm.at[0, j]))
+    finish(stores)
 
 
 def shaped(*shape, dtype=F32):
-    return jax.ShapeDtypeStruct(shape, dtype)
+    return pltpu.HBM(shape, dtype)
 
 
 def all_to_all(value, axes):
     return lax.all_to_all(value, axes, 0, 0, tiled=True)
 
 
-def call(kernel, out, scratch, *args):
+def call(kernel, out, scratch, *args, near=0):
+    args = args[:near] + tuple(pltpu.with_memory_space_constraint(a, pltpu.HBM) for a in args[near:])
     return pl.pallas_call(
         kernel,
         out_shape=out,
-        in_specs=[VMEM_SPEC] * len(args),
-        out_specs=jax.tree.map(lambda _: VMEM_SPEC, out),
+        in_specs=[VMEM_SPEC] * near + [HBM_SPEC] * (len(args) - near),
+        out_specs=jax.tree.map(lambda _: HBM_SPEC, out),
         scratch_shapes=scratch,
         compiler_params=PARAMS,
     )(*args)
@@ -298,21 +404,35 @@
             shaped(n_xy, 288, 2 * feat, dtype=BF16),
             shaped(2 * feat, cols, dtype=BF16),
         ),
-        [VMEM((n_z, feat * rows, 128), F32), VMEM((n_z, feat * rows, 128), F32), VMEM((128, cols), F32)],
+        [
+            VMEM((n_z, feat * rows, 128), F32), VMEM((n_z, feat * rows, 128), F32), VMEM((128, cols), F32),
+            VMEM((2, feat, rows, cols), BF16), VMEM((2, feat, rows, cols), BF16),
+            VMEM((2, rows, cols), jnp.int32), VMEM((rows, cols), jnp.int32), VMEM((rows, cols), jnp.int32),
+            VMEM((2, rows, 2 * feat, cols), BF16), VMEM((n_z, rows, 2 * feat, 128), BF16),
+            VMEM((n_xy, 288, 2 * feat), BF16), DMA((7,)), DMA((8,)),
+        ],
         nodes, upstream, usage, blockage, capacity,
     )
     rim = lax.ppermute(rim, axes, up)
     got_u = all_to_all(sent, "xy")
-    got_v = [lax.ppermute(v, axes, cross_pairs(d)) for d, v in enumerate((v0, v1, v2, v3))]
+    got_v = {d: lax.ppermute((v0, v1, v2, v3)[d], axes, cross_pairs(d)) for d in (2, 1, 3, 0)}
+    got_v = [got_v[d] for d in range(4)]
     weights = (jnp.swapaxes(w_src, 1, 2), jnp.swapaxes(w_dst, 1, 2), w_out)
+    held = [VMEM((2, feat, 128), BF16)] * 3
     ns, back, g_w, g_o = call(
         inside_kernel,
         (
             shaped(2, rows, feat, cols), shaped(feat, cols, dtype=BF16),
             shaped(2, 2 * feat, 128), shaped(2, feat, 128),
         ),
-        [VMEM((3, rows, cols), F32), VMEM((feat, cols), F32)],
-        xd, rim, blockage, capacity, *weights,
+        [
+            VMEM((3, rows, cols), F32), VMEM((feat, cols), F32), VMEM((2, rows, 2 * feat, cols), BF16),
+            VMEM((1, 2, 2, rows, cols), jnp.int32), VMEM((1, 2, 2, rows, cols), jnp.int32), *held,
+            VMEM((2, rows, feat, cols), F32), VMEM((feat, cols), BF16),
+            VMEM((2, 2 * feat, 128), F32), VMEM((2, feat, 128), F32),
+            DMA((5,)), DMA((rows,)), DMA((rows,)), DMA((3,)),
+        ],
+        rim, xd, blockage, capacity, *weights, near=1,
     )
     back = lax.ppermute(back, axes, down)
     gu, gv0, gv1, gv2, gv3 = call(
@@ -324,9 +444,11 @@
         [
             VMEM((n_xy, 256, 128), F32), VMEM((n_z, rows, 2 * feat, 128), BF16),
             VMEM((n_z, rows, feat, 128), BF16), VMEM((32, 128), F32),
-            VMEM((2 * feat, 128), F32), VMEM((feat, 128), F32), VMEM((384, 128), F32),
+            VMEM((2 * feat, 128), F32), VMEM((feat, 128), F32), VMEM((384, 128), F32), *held,
+            VMEM((2, 2 * feat, 128), F32), VMEM((2, feat, 128), F32),
+            VMEM((n_xy, 176, 2 * feat), BF16), DMA((5,)), DMA((5,)),
         ],
-        got_u, *got_v, *weights, g_w, g_o,
+        got_u, *got_v, *weights, g_w, g_o, near=5,
     )
     got_gu = all_to_all(gu, "xy")
     got_gv = [
@@ -338,7 +460,6 @@
     part = got_gu[:, 128:, :].astype(F32).reshape(n_xy, 2, 24, 128)
     part = jnp.broadcast_to(jnp.sum(part, (0, 1))[None], (16, 24, 128))
     part = all_to_all(part, ("l", "z"))
-    part, got_gv[3], back = lax.optimization_barrier((part, got_gv[3], back))
 
     grad_nodes = call(
         finish_kernel,
@@ -346,9 +467,11 @@
         [
             VMEM((n_xy, 128, 128), F32), VMEM((n_z, rows, feat, 128), BF16),
             VMEM((n_z, feat * rows, 128), F32), VMEM((n_z, feat * rows, 128), F32),
-            VMEM((2, rows, cols), F32),
+            VMEM((2, rows, cols), F32), VMEM((2, rows, feat, cols), F32),
+            VMEM((2, rows, 2 * feat, cols), BF16), VMEM((1, 2, rows, cols), jnp.int32),
+            VMEM((2, feat, rows, cols), BF16), DMA((1,)), DMA((rows,)), DMA((rows,)), DMA((2,)),
         ],
-        got_gu, *got_gv, ns, back, xd, usage,
+        got_gu, *got_gv, back, ns, xd, usage, near=6,
     )
     part = jnp.broadcast_to(jnp.sum(part, 0)[None] * scale, (16, 24, 128))
     total = all_to_all(part, "xy").reshape(3, 2, feat, 128)

time: 144 us -> 134 us (0.931)
  the two profiles are of different devices: /device:TPU:34 before, /device:TPU:1 now
where the time goes in v1:
time: 134 us; the launch traced here: 131 us
  blocking collectives  49.9 us (37%)
  starting transfers between devices  39.9 us (30%)
  Pallas kernels  25.5 us (19%)
  waiting for transfers between devices  13.6 us (10%)
  local copies, waits for them, and re-layouts  1.43 us (1%)
    all_to_all x2, blocking collectives, all_to_all(): return lax.all_to_all(value, axes, 0, 0, tiled=True)  49.9 us
    pallas_call x4, Pallas kernels, call(): pl.pallas_call(kernel, out_shape=out, in_specs=[VMEM_SPEC] * near + [HBM_...  25.5 us
    ppermute x4, starting transfers between devices, on_device(): lax.ppermute((v0, v1, v2, v3)[d], axes, cross_pairs(d))  14.2 us
    all_to_all x2, starting transfers between devices, all_to_all(): return lax.all_to_all(value, axes, 0, 0, tiled=True)  11.2 us
    ppermute x4, starting transfers between devices, on_device(): lax.ppermute(g, axes, [(b, a) for a, b in cross_pairs(d)])  10.1 us
    ppermute x4, waiting for transfers between devices, on_device(): lax.ppermute(g, axes, [(b, a) for a, b in cross_pairs(d)])  6.63 us
    ppermute x1, waiting for transfers between devices, on_device(): rim = lax.ppermute(rim, axes, up)  4.89 us
    ppermute x1, starting transfers between devices, on_device(): back = lax.ppermute(back, axes, down)  3.15 us
  transfers between devices with their start and end apart: 12, of which 5 were waited for; matrix products, arithmetic and copies ran while one was open for 0% of the time, Pallas kernels for 11%

profile of v1, /device:TPU:1, one launch (start us, length us, event | category | flops | bytes accessed | tf_op | source)
XLA Modules:
  0.0 131.4 jit_solution(14676161500308191061)
XLA Ops:
  0.6 4.9 %shard_map.111 = (bf16[2,8,128,512]{3,2,1,0:T(8,128)(2,1)}, bf16[8,128,128]{2,1,0:T(8,128)(2,1)}, bf16[8,128,128]{2,1,0:T(8,128)(2,1)}, bf16[8,128,128]{2,1,0:T(...) custom-call(bf16[1,2,64,8,512]{4,3,2,1,0:T(8,128)(2,1)} %nodes_hbm.1, ...), custom_call_target="tpu_custom_call" | custom-call | tf_op jit(solution)/shard_map/pallas_call | solution.py:371
  5.6 7.7 %all-to-all-start = ((bf16[16,288,128]{2,1,0:T(8,128)(2,1)}), bf16[16,288,128]{2,1,0:T(8,128)(2,1)S(1)}, u32[]{:S(2)}, u32[]{:S(2)}) async-start(bf16[16,288,128]{2,1,0:T(8,128)(2,1)} %get-tuple-element.20), calls=%async_computation | async-start | bytes 2359296 | tf_op jit(solution)/shard_map/all_to_all | solution.py:366
  13.3 2.9 %collective-permute-start = (bf16[8,128,128]{2,1,0:T(8,128)(2,1)S(1)}, bf16[8,128,128]{2,1,0:T(8,128)(2,1)S(1)}, u32[]{:S(2)}, u32[]{:S(2)}) collective-permute-start(bf16[8,128,128]{2,1,0:T(8,128)(2,1)S(1)} %copy-done.3), channel_id=1, source_target_pairs={{64,0},{65,1},{66,2},{67,3},{68,4},{69,5},{70,6},{71,7},{72,8},{73... | collective-permute-start | bytes 786440 | tf_op jit(solution)/shard_map/ppermute | solution.py:418
  16.2 4.2 %collective-permute-start.1 = (bf16[8,128,128]{2,1,0:T(8,128)(2,1)S(1)}, bf16[8,128,128]{2,1,0:T(8,128)(2,1)S(1)}, u32[]{:S(2)}, u32[]{:S(2)}) collective-permute-start(bf16[8,128,128]{2,1,0:T(8,128)(2,1)S(1)} %copy-done.2), channel_id=1, source_target_pairs={{64,16},{65,17},{66,18},{67,19},{68,20},{69,21},{70,22},{71,23},{7... | collective-permute-start | bytes 786440 | tf_op jit(solution)/shard_map/ppermute | solution.py:418
  20.4 5.2 %collective-permute-start.2 = (bf16[8,128,128]{2,1,0:T(8,128)(2,1)S(1)}, bf16[8,128,128]{2,1,0:T(8,128)(2,1)S(1)}, u32[]{:S(2)}, u32[]{:S(2)}) collective-permute-start(bf16[8,128,128]{2,1,0:T(8,128)(2,1)S(1)} %copy-done.1), channel_id=1, source_target_pairs={{64,32},{65,33},{66,34},{67,35},{68,36},{69,37},{70,38},{71,39},{7... | collective-permute-start | bytes 786440 | tf_op jit(solution)/shard_map/ppermute | solution.py:418
  25.6 1.9 %collective-permute-start.3 = (bf16[8,128,128]{2,1,0:T(8,128)(2,1)S(1)}, bf16[8,128,128]{2,1,0:T(8,128)(2,1)S(1)}, u32[]{:S(2)}, u32[]{:S(2)}) collective-permute-start(bf16[8,128,128]{2,1,0:T(8,128)(2,1)S(1)} %copy-done), channel_id=1, source_target_pairs={{64,48},{65,49},{66,50},{67,51},{68,52},{69,53},{70,54},{71,55},{7... | collective-permute-start | bytes 786440 | tf_op jit(solution)/shard_map/ppermute | solution.py:418
  27.6 1.3 collective-permute-start.4
  28.9 4.9 %collective-permute-done.4.rim_ref = bf16[128,512]{1,0:T(8,128)(2,1)S(1)} collective-permute-done((bf16[128,512]{1,0:T(8,128)(2,1)S(1)}, bf16[128,512]{1,0:T(8,128)(2,1)S(1)}, u32[]{:S(2)}, u32[]{:S(2)}) %collective-permute-start.4) | collective-permute-done | bytes 131104 | tf_op jit(solution)/shard_map/ppermute | solution.py:416
  33.8 10.8 %shard_map.112 = (f32[2,8,64,512]{3,2,1,0:T(8,128)}, bf16[64,512]{1,0:T(8,128)(2,1)}, f32[2,128,128]{2,1,0:T(8,128)}, f32[2,64,128]{2,1,0:T(8,128)}) custom-call(bf16[128,512]{1,0:T(8,128)(2,1)S(1)} %collective-permute-done.4.rim_ref, bf16[2,8,128,512]{3,2,1,0:T(8,128)(2,1)} %get-tuple-element.26.xd_hbm, s32[1,2,2,8,512]{4,3,2,1,0:T(8,128)} %block_hbm.3, ...), custom_call_target="tpu_custom_call" | custom-call | tf_op jit(solution)/shard_map/pallas_call | solution.py:371
  44.6 0.8 collective-permute-done.3.v3_ref
  45.4 5.6 %shard_map.113 = (bf16[16,176,128]{2,1,0:T(8,128)(2,1)}, bf16[8,64,128]{2,1,0:T(8,128)(2,1)}, bf16[8,64,128]{2,1,0:T(8,128)(2,1)}, bf16[8,64,128]{2,1,0:T(8,128)(2,1)}, bf16[8,64,128]{2,1,0:T(8,128)(2,1)}) custom-call(bf16[16,288,128]{2,1,0:T(8,128)(2,1)S(1)} %all-to-all-done.r_ref, bf16[8,128,128]{2,1,0:T(8,128)(2,1)S(1)} %collective-permute-done.v0_ref, ...), custom_call_target="tpu_custom_call" | custom-call | tf_op jit(solution)/shard_map/pallas_call | solution.py:371
  51.0 22.1 %all_to_all.20.gu_ref = bf16[16,176,128]{2,1,0:T(8,128)(2,1)S(1)} all-to-all(bf16[16,176,128]{2,1,0:T(8,128)(2,1)} %get-tuple-element.29), channel_id=1, replica_groups=mesh['l'=4,'z'=4,'xy'=16] {'xy'}, dimensions={0} | all-to-all | bytes 1441792 | tf_op jit(solution)/shard_map/all_to_all | solution.py:366
  73.2 27.9 %all_to_all.21 = f32[16,24,128]{2,1,0:T(8,128)S(1)} all-to-all(f32[16,24,128]{2,1,0:T(8,128)S(1)} %broadcast_in_dim.4), channel_id=1, replica_groups=mesh['l'=4,'z'=4,'xy'=16] {'l','z'}, dimensions={0} | all-to-all | bytes 393216 | tf_op jit(solution)/shard_map/all_to_all | solution.py:366
  101.1 0.7 broadcast_in_dim.5
  101.8 3.5 %all-to-all-start.3 = ((f32[16,24,128]{2,1,0:T(8,128)}), f32[16,24,128]{2,1,0:T(8,128)S(1)}, u32[]{:S(2)}, u32[]{:S(2)}) async-start(f32[16,24,128]{2,1,0:T(8,128)} %broadcast_in_dim.5), calls=%async_computation.3 | async-start | bytes 393216 | tf_op jit(solution)/shard_map/all_to_all | solution.py:366
  105.3 2.0 %collective-permute-start.5 = (bf16[8,64,128]{2,1,0:T(8,128)(2,1)S(1)}, bf16[8,64,128]{2,1,0:T(8,128)(2,1)S(1)}, u32[]{:S(2)}, u32[]{:S(2)}) collective-permute-start(bf16[8,64,128]{2,1,0:T(8,128)(2,1)S(1)} %copy-done.7), channel_id=1, source_target_pairs={{0,64},{1,65},{2,66},{3,67},{4,68},{5,69},{6,70},{7,71},{8,72},{9,... | collective-permute-start | bytes 393224 | tf_op jit(solution)/shard_map/ppermute | solution.py:455
  107.3 2.3 %collective-permute-start.6 = (bf16[8,64,128]{2,1,0:T(8,128)(2,1)S(1)}, bf16[8,64,128]{2,1,0:T(8,128)(2,1)S(1)}, u32[]{:S(2)}, u32[]{:S(2)}) collective-permute-start(bf16[8,64,128]{2,1,0:T(8,128)(2,1)S(1)} %copy-done.6), channel_id=1, source_target_pairs={{16,64},{17,65},{18,66},{19,67},{20,68},{21,69},{22,70},{23,71},{2... | collective-permute-start | bytes 393224 | tf_op jit(solution)/shard_map/ppermute | solution.py:455
  109.6 3.8 %collective-permute-start.7 = (bf16[8,64,128]{2,1,0:T(8,128)(2,1)S(1)}, bf16[8,64,128]{2,1,0:T(8,128)(2,1)S(1)}, u32[]{:S(2)}, u32[]{:S(2)}) collective-permute-start(bf16[8,64,128]{2,1,0:T(8,128)(2,1)S(1)} %copy-done.5), channel_id=1, source_target_pairs={{32,64},{33,65},{34,66},{35,67},{36,68},{37,69},{38,70},{39,71},{4... | collective-permute-start | bytes 393224 | tf_op jit(solution)/shard_map/ppermute | solution.py:455
  113.4 2.0 %collective-permute-start.8 = (bf16[8,64,128]{2,1,0:T(8,128)(2,1)S(1)}, bf16[8,64,128]{2,1,0:T(8,128)(2,1)S(1)}, u32[]{:S(2)}, u32[]{:S(2)}) collective-permute-start(bf16[8,64,128]{2,1,0:T(8,128)(2,1)S(1)} %copy-done.4), channel_id=1, source_target_pairs={{48,64},{49,65},{50,66},{51,67},{52,68},{53,69},{54,70},{55,71},{5... | collective-permute-start | bytes 393224 | tf_op jit(solution)/shard_map/ppermute | solution.py:455
  115.4 3.1 %collective-permute-start.9 = (bf16[64,512]{1,0:T(8,128)(2,1)S(1)}, bf16[64,512]{1,0:T(8,128)(2,1)S(1)}, u32[]{:S(2)}, u32[]{:S(2)}) collective-permute-start(bf16[64,512]{1,0:T(8,128)(2,1)S(1)} %copy-done.9), channel_id=1, source_target_pairs={{0,1},{1,2},{2,3},{3,4},{4,5},{5,6},{6,7},{7,8},{8,9},{9,10},{10,1... | collective-permute-start | bytes 196616 | tf_op jit(solution)/shard_map/ppermute | solution.py:437
  118.6 1.3 collective-permute-done.9.back_ref
  119.9 4.0 %collective-permute-done.7.gv2_ref = bf16[8,64,128]{2,1,0:T(8,128)(2,1)S(1)} collective-permute-done((bf16[8,64,128]{2,1,0:T(8,128)(2,1)S(1)}, bf16[8,64,128]{2,1,0:T(8,128)(2,1)S(1)}, u32[]{:S(2)}, u32[]{:S(2)}) %collective-permute-start.7) | collective-permute-done | bytes 131104 | tf_op jit(solution)/shard_map/ppermute | solution.py:455
  123.9 2.6 %collective-permute-done.8.gv3_ref = bf16[8,64,128]{2,1,0:T(8,128)(2,1)S(1)} collective-permute-done((bf16[8,64,128]{2,1,0:T(8,128)(2,1)S(1)}, bf16[8,64,128]{2,1,0:T(8,128)(2,1)S(1)}, u32[]{:S(2)}, u32[]{:S(2)}) %collective-permute-start.8) | collective-permute-done | bytes 131104 | tf_op jit(solution)/shard_map/ppermute | solution.py:455
  126.5 4.2 %shard_map.114 = bf16[1,2,64,8,512]{4,3,2,1,0:T(8,128)(2,1)} custom-call(bf16[16,176,128]{2,1,0:T(8,128)(2,1)S(1)} %all_to_all.20.gu_ref, bf16[8,64,128]{2,1,0:T(8,128)(2,1)S(1)} %collective-permute-done.5.gv0_ref, bf16[8,64,128]{2,1,0:T(8,128)(2,1)S(1)} %collective-permute-done.6.gv1_ref, bf16[8,64,128]{2,1,0:T(8,128)(2,1)S(1)} %collective-permute-done.7.gv2_ref, ...), custom_call_target="tpu_custom_call" | custom-call | tf_op jit(solution)/shard_map/pallas_call | solution.py:371
  (33 shorter events, 0.8 us)
Async XLA Ops:
  5.6 7.8 %copy-start.3 = (bf16[8,128,128]{2,1,0:T(8,128)(2,1)S(1)}, bf16[8,128,128]{2,1,0:T(8,128)(2,1)}, u32[]{:S(2)}) copy-start(bf16[8,128,128]{2,1,0:T(8,128)(2,1)} %get-tuple-element.21) | copy-start | bytes 786436
  5.6 10.6 %copy-start.2 = (bf16[8,128,128]{2,1,0:T(8,128)(2,1)S(1)}, bf16[8,128,128]{2,1,0:T(8,128)(2,1)}, u32[]{:S(2)}) copy-start(bf16[8,128,128]{2,1,0:T(8,128)(2,1)} %get-tuple-element.22) | copy-start | bytes 786436
  5.6 14.8 %copy-start.1 = (bf16[8,128,128]{2,1,0:T(8,128)(2,1)S(1)}, bf16[8,128,128]{2,1,0:T(8,128)(2,1)}, u32[]{:S(2)}) copy-start(bf16[8,128,128]{2,1,0:T(8,128)(2,1)} %get-tuple-element.23) | copy-start | bytes 786436
  5.6 20.0 %copy-start = (bf16[8,128,128]{2,1,0:T(8,128)(2,1)S(1)}, bf16[8,128,128]{2,1,0:T(8,128)(2,1)}, u32[]{:S(2)}) copy-start(bf16[8,128,128]{2,1,0:T(8,128)(2,1)} %get-tuple-element.24) | copy-start | bytes 786436
  5.6 22.0 %copy-start.8 = (bf16[128,512]{1,0:T(8,128)(2,1)S(1)}, bf16[128,512]{1,0:T(8,128)(2,1)}, u32[]{:S(2)}) copy-start(bf16[128,512]{1,0:T(8,128)(2,1)} %get-tuple-element.25) | copy-start | bytes 393220
  5.6 39.8 %all-to-all-start = ((bf16[16,288,128]{2,1,0:T(8,128)(2,1)}), bf16[16,288,128]{2,1,0:T(8,128)(2,1)S(1)}, u32[]{:S(2)}, u32[]{:S(2)}) async-start(bf16[16,288,128]{2,1,0:T(8,128)(2,1)} %get-tuple-element.20), calls=%async_computation | async-start | bytes 2359296 | tf_op jit(solution)/shard_map/all_to_all | solution.py:366
  13.3 31.3 %collective-permute-start = (bf16[8,128,128]{2,1,0:T(8,128)(2,1)S(1)}, bf16[8,128,128]{2,1,0:T(8,128)(2,1)S(1)}, u32[]{:S(2)}, u32[]{:S(2)}) collective-permute-start(bf16[8,128,128]{2,1,0:T(8,128)(2,1)S(1)} %copy-done.3), channel_id=1, source_target_pairs={{64,0},{65,1},{66,2},{67,3},{68,4},{69,5},{70,6},{71,7},{72,8},{73... | collective-permute-start | bytes 786440 | tf_op jit(solution)/shard_map/ppermute | solution.py:418
  16.2 28.4 %collective-permute-start.1 = (bf16[8,128,128]{2,1,0:T(8,128)(2,1)S(1)}, bf16[8,128,128]{2,1,0:T(8,128)(2,1)S(1)}, u32[]{:S(2)}, u32[]{:S(2)}) collective-permute-start(bf16[8,128,128]{2,1,0:T(8,128)(2,1)S(1)} %copy-done.2), channel_id=1, source_target_pairs={{64,16},{65,17},{66,18},{67,19},{68,20},{69,21},{70,22},{71,23},{7... | collective-permute-start | bytes 786440 | tf_op jit(solution)/shard_map/ppermute | solution.py:418
  20.4 24.2 %collective-permute-start.2 = (bf16[8,128,128]{2,1,0:T(8,128)(2,1)S(1)}, bf16[8,128,128]{2,1,0:T(8,128)(2,1)S(1)}, u32[]{:S(2)}, u32[]{:S(2)}) collective-permute-start(bf16[8,128,128]{2,1,0:T(8,128)(2,1)S(1)} %copy-done.1), channel_id=1, source_target_pairs={{64,32},{65,33},{66,34},{67,35},{68,36},{69,37},{70,38},{71,39},{7... | collective-permute-start | bytes 786440 | tf_op jit(solution)/shard_map/ppermute | solution.py:418
  25.6 19.8 %collective-permute-start.3 = (bf16[8,128,128]{2,1,0:T(8,128)(2,1)S(1)}, bf16[8,128,128]{2,1,0:T(8,128)(2,1)S(1)}, u32[]{:S(2)}, u32[]{:S(2)}) collective-permute-start(bf16[8,128,128]{2,1,0:T(8,128)(2,1)S(1)} %copy-done), channel_id=1, source_target_pairs={{64,48},{65,49},{66,50},{67,51},{68,52},{69,53},{70,54},{71,55},{7... | collective-permute-start | bytes 786440 | tf_op jit(solution)/shard_map/ppermute | solution.py:418
  27.6 6.2 %collective-permute-start.4 = (bf16[128,512]{1,0:T(8,128)(2,1)S(1)}, bf16[128,512]{1,0:T(8,128)(2,1)S(1)}, u32[]{:S(2)}, u32[]{:S(2)}) collective-permute-start(bf16[128,512]{1,0:T(8,128)(2,1)S(1)} %copy-done.8), channel_id=1, source_target_pairs={{1,0},{2,1},{3,2},{4,3},{5,4},{6,5},{7,6},{8,7},{9,8},{10,9},{11,1... | collective-permute-start | bytes 393224 | tf_op jit(solution)/shard_map/ppermute | solution.py:416
  51.0 54.3 %copy-start.7 = (bf16[8,64,128]{2,1,0:T(8,128)(2,1)S(1)}, bf16[8,64,128]{2,1,0:T(8,128)(2,1)}, u32[]{:S(2)}) copy-start(bf16[8,64,128]{2,1,0:T(8,128)(2,1)} %get-tuple-element.30) | copy-start | bytes 393220
  51.0 56.4 %copy-start.6 = (bf16[8,64,128]{2,1,0:T(8,128)(2,1)S(1)}, bf16[8,64,128]{2,1,0:T(8,128)(2,1)}, u32[]{:S(2)}) copy-start(bf16[8,64,128]{2,1,0:T(8,128)(2,1)} %get-tuple-element.31) | copy-start | bytes 393220
  51.0 58.6 %copy-start.5 = (bf16[8,64,128]{2,1,0:T(8,128)(2,1)S(1)}, bf16[8,64,128]{2,1,0:T(8,128)(2,1)}, u32[]{:S(2)}) copy-start(bf16[8,64,128]{2,1,0:T(8,128)(2,1)} %get-tuple-element.32) | copy-start | bytes 393220
  51.0 62.4 %copy-start.4 = (bf16[8,64,128]{2,1,0:T(8,128)(2,1)S(1)}, bf16[8,64,128]{2,1,0:T(8,128)(2,1)}, u32[]{:S(2)}) copy-start(bf16[8,64,128]{2,1,0:T(8,128)(2,1)} %get-tuple-element.33) | copy-start | bytes 393220
  51.0 64.4 %copy-start.9 = (bf16[64,512]{1,0:T(8,128)(2,1)S(1)}, bf16[64,512]{1,0:T(8,128)(2,1)}, u32[]{:S(2)}) copy-start(bf16[64,512]{1,0:T(8,128)(2,1)} %get-tuple-element.34) | copy-start | bytes 196612
  101.8 29.0 %all-to-all-start.3 = ((f32[16,24,128]{2,1,0:T(8,128)}), f32[16,24,128]{2,1,0:T(8,128)S(1)}, u32[]{:S(2)}, u32[]{:S(2)}) async-start(f32[16,24,128]{2,1,0:T(8,128)} %broadcast_in_dim.5), calls=%async_computation.3 | async-start | bytes 393216 | tf_op jit(solution)/shard_map/all_to_all | solution.py:366
  105.3 14.6 %collective-permute-start.5 = (bf16[8,64,128]{2,1,0:T(8,128)(2,1)S(1)}, bf16[8,64,128]{2,1,0:T(8,128)(2,1)S(1)}, u32[]{:S(2)}, u32[]{:S(2)}) collective-permute-start(bf16[8,64,128]{2,1,0:T(8,128)(2,1)S(1)} %copy-done.7), channel_id=1, source_target_pairs={{0,64},{1,65},{2,66},{3,67},{4,68},{5,69},{6,70},{7,71},{8,72},{9,... | collective-permute-start | bytes 393224 | tf_op jit(solution)/shard_map/ppermute | solution.py:455
  107.3 12.6 %collective-permute-start.6 = (bf16[8,64,128]{2,1,0:T(8,128)(2,1)S(1)}, bf16[8,64,128]{2,1,0:T(8,128)(2,1)S(1)}, u32[]{:S(2)}, u32[]{:S(2)}) collective-permute-start(bf16[8,64,128]{2,1,0:T(8,128)(2,1)S(1)} %copy-done.6), channel_id=1, source_target_pairs={{16,64},{17,65},{18,66},{19,67},{20,68},{21,69},{22,70},{23,71},{2... | collective-permute-start | bytes 393224 | tf_op jit(solution)/shard_map/ppermute | solution.py:455
  109.6 14.2 %collective-permute-start.7 = (bf16[8,64,128]{2,1,0:T(8,128)(2,1)S(1)}, bf16[8,64,128]{2,1,0:T(8,128)(2,1)S(1)}, u32[]{:S(2)}, u32[]{:S(2)}) collective-permute-start(bf16[8,64,128]{2,1,0:T(8,128)(2,1)S(1)} %copy-done.5), channel_id=1, source_target_pairs={{32,64},{33,65},{34,66},{35,67},{36,68},{37,69},{38,70},{39,71},{4... | collective-permute-start | bytes 393224 | tf_op jit(solution)/shard_map/ppermute | solution.py:455
  113.4 13.1 %collective-permute-start.8 = (bf16[8,64,128]{2,1,0:T(8,128)(2,1)S(1)}, bf16[8,64,128]{2,1,0:T(8,128)(2,1)S(1)}, u32[]{:S(2)}, u32[]{:S(2)}) collective-permute-start(bf16[8,64,128]{2,1,0:T(8,128)(2,1)S(1)} %copy-done.4), channel_id=1, source_target_pairs={{48,64},{49,65},{50,66},{51,67},{52,68},{53,69},{54,70},{55,71},{5... | collective-permute-start | bytes 393224 | tf_op jit(solution)/shard_map/ppermute | solution.py:455
  115.4 4.5 %collective-permute-start.9 = (bf16[64,512]{1,0:T(8,128)(2,1)S(1)}, bf16[64,512]{1,0:T(8,128)(2,1)S(1)}, u32[]{:S(2)}, u32[]{:S(2)}) collective-permute-start(bf16[64,512]{1,0:T(8,128)(2,1)S(1)} %copy-done.9), channel_id=1, source_target_pairs={{0,1},{1,2},{2,3},{3,4},{4,5},{5,6},{6,7},{7,8},{8,9},{9,10},{10,1... | collective-permute-start | bytes 196616 | tf_op jit(solution)/shard_map/ppermute | solution.py:437

commit v2 on v1

--- a/solution.py
+++ b/solution.py
@@ -100,7 +100,7 @@
             )
 
         if j == 0:
-            @pl.loop(0, rows)
+            @pl.loop(0, rows, unroll=4)
             def _(r):
                 xd_ref[0, r] = row_of(r).astype(BF16)
                 for d in range(zs):
@@ -116,7 +116,7 @@
                 (v_ref.at[3], v3_hbm),
             )
         else:
-            @pl.loop(0, rows // 2)
+            @pl.loop(0, rows // 2, unroll=2)
             def _(half):
                 pieces = []
                 for k in range(2):
@@ -203,20 +203,22 @@
         ns_ref[1, r] = g_x[feat:]
         own = xd_ref[col_layer, r].astype(F32)
         side = pltpu.roll(own, cols - 1, 1)
-        x_uv = jnp.concatenate((own[:feat], side[:feat]), 0).astype(BF16)
-        g_x, g_w, g_o = edges(planar, x_uv, side[feat:] - own[feat:], gates[0, pl.ds(r, 1), :])
+        x_col = jnp.concatenate((own[:feat], side[:feat]), 0).astype(BF16)
+        low = xd_ref[row_layer, r]
+        high = jnp.where(r == rows - 1, rim_ref[...], xd_ref[row_layer, jnp.minimum(r + 1, rows - 1)])
+        x_row = jnp.concatenate((low[:feat], high[:feat]), 0)
+        diff = high[feat:].astype(F32) - low[feat:].astype(F32)
+        g_x, g_w, g_o = edges(
+            planar,
+            jnp.concatenate((x_col, x_row), 1),
+            jnp.concatenate((side[feat:] - own[feat:], diff), 1),
+            jnp.concatenate((gates[0, pl.ds(r, 1), :], gates[2, pl.ds(r, 1), :]), 1),
+        )
         g_w_ref[0] += g_w
         g_o_ref[0] += g_o
-        ns_ref[col_layer, r] += g_x[:feat] + pltpu.roll(g_x[feat:], 1, 1)
-        low = xd_ref[row_layer, r]
-        high = jnp.where(r == rows - 1, rim_ref[...], xd_ref[row_layer, jnp.minimum(r + 1, rows - 1)])
-        x_uv = jnp.concatenate((low[:feat], high[:feat]), 0)
-        diff = high[feat:].astype(F32) - low[feat:].astype(F32)
-        g_x, g_w, g_o = edges(planar, x_uv, diff, gates[2, pl.ds(r, 1), :])
-        g_w_ref[0] += g_w
-        g_o_ref[0] += g_o
-        ns_ref[row_layer, r] += carry[...] + g_x[:feat]
-        carry[...] = g_x[feat:]
+        ns_ref[col_layer, r] += g_x[:feat, :cols] + pltpu.roll(g_x[feat:, :cols], 1, 1)
+        ns_ref[row_layer, r] += carry[...] + g_x[:feat, cols:]
+        carry[...] = g_x[feat:, cols:]
         row_out(r).start()
 
     back_ref[...] = carry[...].astype(BF16)
@@ -249,7 +251,7 @@
     finish(loads)
     via = load_weights(w_src_ref, w_dst_ref, w_out_ref, 1)
 
-    @pl.loop(0, 8, unroll=2)
+    @pl.loop(0, 8, unroll=4)
     def _(i):
         z2 = i // 4
         c2 = lax.rem(i, 4)
@@ -327,7 +329,7 @@
         gvs[lax.rem(z + d, zs)] = gv_ref[...]
     damps[...] = lax.rsqrt(1.0 + usage_ref[0].astype(F32))
 
-    @pl.loop(0, rows, unroll=2)
+    @pl.loop(0, rows, unroll=4)
     def _(r):
         finish(rows_in(r))
 
@@ -460,6 +462,7 @@
     part = got_gu[:, 128:, :].astype(F32).reshape(n_xy, 2, 24, 128)
     part = jnp.broadcast_to(jnp.sum(part, (0, 1))[None], (16, 24, 128))
     part = all_to_all(part, ("l", "z"))
+    part, got_gv[0] = lax.optimization_barrier((part, got_gv[0]))
 
     grad_nodes = call(
         finish_kernel,

time: 134 us -> 133 us (level)
  the two profiles are of different devices: /device:TPU:1 before, /device:TPU:64 now
where the time goes in v2:
time: 133 us; the launch traced here: 132 us
  starting transfers between devices  58.5 us (44%)
  Pallas kernels  24.3 us (18%)
  blocking collectives  23 us (17%)
  waiting for transfers between devices  22.9 us (17%)
  local copies, waits for them, and re-layouts  2.11 us (2%)
    all_to_all x3, starting transfers between devices, all_to_all(): return lax.all_to_all(value, axes, 0, 0, tiled=True)  29.8 us
    pallas_call x4, Pallas kernels, call(): pl.pallas_call(kernel, out_shape=out, in_specs=[VMEM_SPEC] * near + [HBM_...  24.3 us
    all_to_all x1, blocking collectives, all_to_all(): return lax.all_to_all(value, axes, 0, 0, tiled=True)  23 us
    ppermute x4, starting transfers between devices, on_device(): lax.ppermute(g, axes, [(b, a) for a, b in cross_pairs(d)])  13.8 us
    ppermute x1, waiting for transfers between devices, on_device(): back = lax.ppermute(back, axes, down)  9.97 us
    ppermute x1, waiting for transfers between devices, on_device(): rim = lax.ppermute(rim, axes, up)  6.25 us
    ppermute x1, starting transfers between devices, on_device(): rim = lax.ppermute(rim, axes, up)  6.25 us
    all_to_all x3, waiting for transfers between devices, all_to_all(): return lax.all_to_all(value, axes, 0, 0, tiled=True)  5.65 us
  transfers between devices with their start and end apart: 13, of which 4 were waited for; matrix products, arithmetic and copies ran while one was open for 0% of the time, Pallas kernels for 11%

profile of v2, /device:TPU:64, one launch (start us, length us, event | category | flops | bytes accessed | tf_op | source)
XLA Modules:
  0.0 131.8 jit_solution(15793281215398479123)
XLA Ops:
  0.6 4.6 %shard_map.111 = (bf16[2,8,128,512]{3,2,1,0:T(8,128)(2,1)}, bf16[8,128,128]{2,1,0:T(8,128)(2,1)}, bf16[8,128,128]{2,1,0:T(8,128)(2,1)}, bf16[8,128,128]{2,1,0:T(...) custom-call(bf16[1,2,64,8,512]{4,3,2,1,0:T(8,128)(2,1)} %nodes_hbm.1, ...), custom_call_target="tpu_custom_call" | custom-call | tf_op jit(solution)/shard_map/pallas_call | solution.py:373
  5.3 7.2 %all-to-all-start = ((bf16[16,288,128]{2,1,0:T(8,128)(2,1)}), bf16[16,288,128]{2,1,0:T(8,128)(2,1)S(1)}, u32[]{:S(2)}, u32[]{:S(2)}) async-start(bf16[16,288,128]{2,1,0:T(8,128)(2,1)} %get-tuple-element.22), calls=%async_computation | async-start | bytes 2359296 | tf_op jit(solution)/shard_map/all_to_all | solution.py:368
  12.5 1.3 collective-permute-start
  13.8 1.3 collective-permute-start.1
  15.1 1.3 collective-permute-start.2
  16.4 1.3 collective-permute-start.3
  17.8 6.2 %collective-permute-start.4 = (bf16[128,512]{1,0:T(8,128)(2,1)S(1)}, bf16[128,512]{1,0:T(8,128)(2,1)S(1)}, u32[]{:S(2)}, u32[]{:S(2)}) collective-permute-start(bf16[128,512]{1,0:T(8,128)(2,1)S(1)} %copy-done.7), channel_id=1, source_target_pairs={{1,0},{2,1},{3,2},{4,3},{5,4},{6,5},{7,6},{8,7},{9,8},{10,9},{11,1... | collective-permute-start | bytes 393224 | tf_op jit(solution)/shard_map/ppermute | solution.py:418
  24.0 6.3 %collective-permute-done.4.rim_ref = bf16[128,512]{1,0:T(8,128)(2,1)S(1)} collective-permute-done((bf16[128,512]{1,0:T(8,128)(2,1)S(1)}, bf16[128,512]{1,0:T(8,128)(2,1)S(1)}, u32[]{:S(2)}, u32[]{:S(2)}) %collective-permute-start.4) | collective-permute-done | bytes 131104 | tf_op jit(solution)/shard_map/ppermute | solution.py:418
  30.3 10.5 %shard_map.112 = (f32[2,8,64,512]{3,2,1,0:T(8,128)}, bf16[64,512]{1,0:T(8,128)(2,1)}, f32[2,128,128]{2,1,0:T(8,128)}, f32[2,64,128]{2,1,0:T(8,128)}) custom-call(bf16[128,512]{1,0:T(8,128)(2,1)S(1)} %collective-permute-done.4.rim_ref, bf16[2,8,128,512]{3,2,1,0:T(8,128)(2,1)} %get-tuple-element.28.xd_hbm, s32[1,2,2,8,512]{4,3,2,1,0:T(8,128)} %block_hbm.3, ...), custom_call_target="tpu_custom_call" | custom-call | tf_op jit(solution)/shard_map/pallas_call | solution.py:373
  40.8 5.0 %shard_map.113 = (bf16[16,176,128]{2,1,0:T(8,128)(2,1)}, bf16[8,64,128]{2,1,0:T(8,128)(2,1)}, bf16[8,64,128]{2,1,0:T(8,128)(2,1)}, bf16[8,64,128]{2,1,0:T(8,128)(2,1)}, bf16[8,64,128]{2,1,0:T(8,128)(2,1)}) custom-call(bf16[16,288,128]{2,1,0:T(8,128)(2,1)S(1)} %all-to-all-done.r_ref, bf16[8,128,128]{2,1,0:T(8,128)(2,1)S(1)} %collective-permute-done.v0_ref, ...), custom_call_target="tpu_custom_call" | custom-call | tf_op jit(solution)/shard_map/pallas_call | solution.py:373
  45.9 23.0 %all_to_all.20.gu_ref = bf16[16,176,128]{2,1,0:T(8,128)(2,1)S(1)} all-to-all(bf16[16,176,128]{2,1,0:T(8,128)(2,1)} %get-tuple-element.31), channel_id=1, replica_groups=mesh['l'=4,'z'=4,'xy'=16] {'xy'}, dimensions={0} | all-to-all | bytes 1441792 | tf_op jit(solution)/shard_map/all_to_all | solution.py:368
  68.9 0.7 broadcast_in_dim.4
  69.6 19.1 %all-to-all-start.2 = ((f32[16,24,128]{2,1,0:T(8,128)}), f32[16,24,128]{2,1,0:T(8,128)S(1)}, u32[]{:S(2)}, u32[]{:S(2)}) async-start(f32[16,24,128]{2,1,0:T(8,128)} %broadcast_in_dim.4), calls=%async_computation.2 | async-start | bytes 393216 | tf_op jit(solution)/shard_map/all_to_all | solution.py:368
  88.6 2.0 %collective-permute-start.5 = (bf16[8,64,128]{2,1,0:T(8,128)(2,1)S(1)}, bf16[8,64,128]{2,1,0:T(8,128)(2,1)S(1)}, u32[]{:S(2)}, u32[]{:S(2)}) collective-permute-start(bf16[8,64,128]{2,1,0:T(8,128)(2,1)S(1)} %copy-done.8), channel_id=1, source_target_pairs={{0,64},{1,65},{2,66},{3,67},{4,68},{5,69},{6,70},{7,71},{8,72},{9,... | collective-permute-start | bytes 393224 | tf_op jit(solution)/shard_map/ppermute | solution.py:457
  90.7 1.0 collective-permute-done.5.gv0_ref
  91.6 5.6 %all-to-all-done.2 = f32[16,24,128]{2,1,0:T(8,128)S(1)} async-done(((f32[16,24,128]{2,1,0:T(8,128)}), f32[16,24,128]{2,1,0:T(8,128)S(1)}, u32[]{:S(2)}, u32[]{:S(2)}) %all-to-all-start.2) | async-done | bytes 196640 | tf_op jit(solution)/shard_map/all_to_all | solution.py:368
  97.3 0.7 broadcast_in_dim.5
  98.0 3.6 %all-to-all-start.3 = ((f32[16,24,128]{2,1,0:T(8,128)}), f32[16,24,128]{2,1,0:T(8,128)S(1)}, u32[]{:S(2)}, u32[]{:S(2)}) async-start(f32[16,24,128]{2,1,0:T(8,128)} %broadcast_in_dim.5), calls=%async_computation.3 | async-start | bytes 393216 | tf_op jit(solution)/shard_map/all_to_all | solution.py:368
  101.6 4.4 %collective-permute-start.6 = (bf16[8,64,128]{2,1,0:T(8,128)(2,1)S(1)}, bf16[8,64,128]{2,1,0:T(8,128)(2,1)S(1)}, u32[]{:S(2)}, u32[]{:S(2)}) collective-permute-start(bf16[8,64,128]{2,1,0:T(8,128)(2,1)S(1)} %copy-done.6), channel_id=1, source_target_pairs={{16,64},{17,65},{18,66},{19,67},{20,68},{21,69},{22,70},{23,71},{2... | collective-permute-start | bytes 393224 | tf_op jit(solution)/shard_map/ppermute | solution.py:457
  106.0 3.8 %collective-permute-start.7 = (bf16[8,64,128]{2,1,0:T(8,128)(2,1)S(1)}, bf16[8,64,128]{2,1,0:T(8,128)(2,1)S(1)}, u32[]{:S(2)}, u32[]{:S(2)}) collective-permute-start(bf16[8,64,128]{2,1,0:T(8,128)(2,1)S(1)} %copy-done.5), channel_id=1, source_target_pairs={{32,64},{33,65},{34,66},{35,67},{36,68},{37,69},{38,70},{39,71},{4... | collective-permute-start | bytes 393224 | tf_op jit(solution)/shard_map/ppermute | solution.py:457
  109.8 3.6 %collective-permute-start.8 = (bf16[8,64,128]{2,1,0:T(8,128)(2,1)S(1)}, bf16[8,64,128]{2,1,0:T(8,128)(2,1)S(1)}, u32[]{:S(2)}, u32[]{:S(2)}) collective-permute-start(bf16[8,64,128]{2,1,0:T(8,128)(2,1)S(1)} %copy-done.4), channel_id=1, source_target_pairs={{48,64},{49,65},{50,66},{51,67},{52,68},{53,69},{54,70},{55,71},{5... | collective-permute-start | bytes 393224 | tf_op jit(solution)/shard_map/ppermute | solution.py:457
  113.5 3.4 %collective-permute-start.9 = (bf16[64,512]{1,0:T(8,128)(2,1)S(1)}, bf16[64,512]{1,0:T(8,128)(2,1)S(1)}, u32[]{:S(2)}, u32[]{:S(2)}) collective-permute-start(bf16[64,512]{1,0:T(8,128)(2,1)S(1)} %copy-done.9), channel_id=1, source_target_pairs={{0,1},{1,2},{2,3},{3,4},{4,5},{5,6},{6,7},{7,8},{8,9},{9,10},{10,1... | collective-permute-start | bytes 196616 | tf_op jit(solution)/shard_map/ppermute | solution.py:439
  116.9 10.0 %collective-permute-done.9.back_ref = bf16[64,512]{1,0:T(8,128)(2,1)S(1)} collective-permute-done((bf16[64,512]{1,0:T(8,128)(2,1)S(1)}, bf16[64,512]{1,0:T(8,128)(2,1)S(1)}, u32[]{:S(2)}, u32[]{:S(2)}) %collective-permute-start.9) | collective-permute-done | bytes 65568 | tf_op jit(solution)/shard_map/ppermute | solution.py:439
  126.9 4.2 %shard_map.114 = bf16[1,2,64,8,512]{4,3,2,1,0:T(8,128)(2,1)} custom-call(bf16[16,176,128]{2,1,0:T(8,128)(2,1)S(1)} %all_to_all.20.gu_ref, bf16[8,64,128]{2,1,0:T(8,128)(2,1)S(1)} %collective-permute-done.5.gv0_ref, bf16[8,64,128]{2,1,0:T(8,128)(2,1)S(1)} %collective-permute-done.6.gv1_ref, bf16[8,64,128]{2,1,0:T(8,128)(2,1)S(1)} %collective-permute-done.7.gv2_ref, ...), custom_call_target="tpu_custom_call" | custom-call | tf_op jit(solution)/shard_map/pallas_call | solution.py:373
  (34 shorter events, 0.8 us)
Async XLA Ops:
  5.3 7.2 %copy-start.3 = (bf16[8,128,128]{2,1,0:T(8,128)(2,1)S(1)}, bf16[8,128,128]{2,1,0:T(8,128)(2,1)}, u32[]{:S(2)}) copy-start(bf16[8,128,128]{2,1,0:T(8,128)(2,1)} %get-tuple-element.23) | copy-start | bytes 786436
  5.3 8.5 %copy-start.2 = (bf16[8,128,128]{2,1,0:T(8,128)(2,1)S(1)}, bf16[8,128,128]{2,1,0:T(8,128)(2,1)}, u32[]{:S(2)}) copy-start(bf16[8,128,128]{2,1,0:T(8,128)(2,1)} %get-tuple-element.24) | copy-start | bytes 786436
  5.3 9.8 %copy-start.1 = (bf16[8,128,128]{2,1,0:T(8,128)(2,1)S(1)}, bf16[8,128,128]{2,1,0:T(8,128)(2,1)}, u32[]{:S(2)}) copy-start(bf16[8,128,128]{2,1,0:T(8,128)(2,1)} %get-tuple-element.25) | copy-start | bytes 786436
  5.3 11.1 %copy-start = (bf16[8,128,128]{2,1,0:T(8,128)(2,1)S(1)}, bf16[8,128,128]{2,1,0:T(8,128)(2,1)}, u32[]{:S(2)}) copy-start(bf16[8,128,128]{2,1,0:T(8,128)(2,1)} %get-tuple-element.26) | copy-start | bytes 786436
  5.3 12.4 %copy-start.7 = (bf16[128,512]{1,0:T(8,128)(2,1)S(1)}, bf16[128,512]{1,0:T(8,128)(2,1)}, u32[]{:S(2)}) copy-start(bf16[128,512]{1,0:T(8,128)(2,1)} %get-tuple-element.27) | copy-start | bytes 393220
  5.3 35.5 %all-to-all-start = ((bf16[16,288,128]{2,1,0:T(8,128)(2,1)}), bf16[16,288,128]{2,1,0:T(8,128)(2,1)S(1)}, u32[]{:S(2)}, u32[]{:S(2)}) async-start(bf16[16,288,128]{2,1,0:T(8,128)(2,1)} %get-tuple-element.22), calls=%async_computation | async-start | bytes 2359296 | tf_op jit(solution)/shard_map/all_to_all | solution.py:368
  12.5 28.3 %collective-permute-start = (bf16[8,128,128]{2,1,0:T(8,128)(2,1)S(1)}, bf16[8,128,128]{2,1,0:T(8,128)(2,1)S(1)}, u32[]{:S(2)}, u32[]{:S(2)}) collective-permute-start(bf16[8,128,128]{2,1,0:T(8,128)(2,1)S(1)} %copy-done.3), channel_id=1, source_target_pairs={{64,0},{65,1},{66,2},{67,3},{68,4},{69,5},{70,6},{71,7},{72,8},{73... | collective-permute-start | bytes 786440 | tf_op jit(solution)/shard_map/ppermute | solution.py:420
  13.8 27.0 %collective-permute-start.1 = (bf16[8,128,128]{2,1,0:T(8,128)(2,1)S(1)}, bf16[8,128,128]{2,1,0:T(8,128)(2,1)S(1)}, u32[]{:S(2)}, u32[]{:S(2)}) collective-permute-start(bf16[8,128,128]{2,1,0:T(8,128)(2,1)S(1)} %copy-done.2), channel_id=1, source_target_pairs={{64,16},{65,17},{66,18},{67,19},{68,20},{69,21},{70,22},{71,23},{7... | collective-permute-start | bytes 786440 | tf_op jit(solution)/shard_map/ppermute | solution.py:420
  15.1 25.7 %collective-permute-start.2 = (bf16[8,128,128]{2,1,0:T(8,128)(2,1)S(1)}, bf16[8,128,128]{2,1,0:T(8,128)(2,1)S(1)}, u32[]{:S(2)}, u32[]{:S(2)}) collective-permute-start(bf16[8,128,128]{2,1,0:T(8,128)(2,1)S(1)} %copy-done.1), channel_id=1, source_target_pairs={{64,32},{65,33},{66,34},{67,35},{68,36},{69,37},{70,38},{71,39},{7... | collective-permute-start | bytes 786440 | tf_op jit(solution)/shard_map/ppermute | solution.py:420
  16.4 24.4 %collective-permute-start.3 = (bf16[8,128,128]{2,1,0:T(8,128)(2,1)S(1)}, bf16[8,128,128]{2,1,0:T(8,128)(2,1)S(1)}, u32[]{:S(2)}, u32[]{:S(2)}) collective-permute-start(bf16[8,128,128]{2,1,0:T(8,128)(2,1)S(1)} %copy-done), channel_id=1, source_target_pairs={{64,48},{65,49},{66,50},{67,51},{68,52},{69,53},{70,54},{71,55},{7... | collective-permute-start | bytes 786440 | tf_op jit(solution)/shard_map/ppermute | solution.py:420
  17.8 12.5 %collective-permute-start.4 = (bf16[128,512]{1,0:T(8,128)(2,1)S(1)}, bf16[128,512]{1,0:T(8,128)(2,1)S(1)}, u32[]{:S(2)}, u32[]{:S(2)}) collective-permute-start(bf16[128,512]{1,0:T(8,128)(2,1)S(1)} %copy-done.7), channel_id=1, source_target_pairs={{1,0},{2,1},{3,2},{4,3},{5,4},{6,5},{7,6},{8,7},{9,8},{10,9},{11,1... | collective-permute-start | bytes 393224 | tf_op jit(solution)/shard_map/ppermute | solution.py:418
  45.8 42.8 %copy-start.8 = (bf16[8,64,128]{2,1,0:T(8,128)(2,1)S(1)}, bf16[8,64,128]{2,1,0:T(8,128)(2,1)}, u32[]{:S(2)}) copy-start(bf16[8,64,128]{2,1,0:T(8,128)(2,1)} %get-tuple-element.32) | copy-start | bytes 393220
  45.8 55.8 %copy-start.6 = (bf16[8,64,128]{2,1,0:T(8,128)(2,1)S(1)}, bf16[8,64,128]{2,1,0:T(8,128)(2,1)}, u32[]{:S(2)}) copy-start(bf16[8,64,128]{2,1,0:T(8,128)(2,1)} %get-tuple-element.34) | copy-start | bytes 393220
  45.8 60.2 %copy-start.5 = (bf16[8,64,128]{2,1,0:T(8,128)(2,1)S(1)}, bf16[8,64,128]{2,1,0:T(8,128)(2,1)}, u32[]{:S(2)}) copy-start(bf16[8,64,128]{2,1,0:T(8,128)(2,1)} %get-tuple-element.35) | copy-start | bytes 393220
  45.8 64.0 %copy-start.4 = (bf16[8,64,128]{2,1,0:T(8,128)(2,1)S(1)}, bf16[8,64,128]{2,1,0:T(8,128)(2,1)}, u32[]{:S(2)}) copy-start(bf16[8,64,128]{2,1,0:T(8,128)(2,1)} %get-tuple-element.36) | copy-start | bytes 393220
  45.8 67.6 %copy-start.9 = (bf16[64,512]{1,0:T(8,128)(2,1)S(1)}, bf16[64,512]{1,0:T(8,128)(2,1)}, u32[]{:S(2)}) copy-start(bf16[64,512]{1,0:T(8,128)(2,1)} %get-tuple-element.37) | copy-start | bytes 196612
  69.6 27.7 %all-to-all-start.2 = ((f32[16,24,128]{2,1,0:T(8,128)}), f32[16,24,128]{2,1,0:T(8,128)S(1)}, u32[]{:S(2)}, u32[]{:S(2)}) async-start(f32[16,24,128]{2,1,0:T(8,128)} %broadcast_in_dim.4), calls=%async_computation.2 | async-start | bytes 393216 | tf_op jit(solution)/shard_map/all_to_all | solution.py:368
  88.6 3.0 %collective-permute-start.5 = (bf16[8,64,128]{2,1,0:T(8,128)(2,1)S(1)}, bf16[8,64,128]{2,1,0:T(8,128)(2,1)S(1)}, u32[]{:S(2)}, u32[]{:S(2)}) collective-permute-start(bf16[8,64,128]{2,1,0:T(8,128)(2,1)S(1)} %copy-done.8), channel_id=1, source_target_pairs={{0,64},{1,65},{2,66},{3,67},{4,68},{5,69},{6,70},{7,71},{8,72},{9,... | collective-permute-start | bytes 393224 | tf_op jit(solution)/shard_map/ppermute | solution.py:457
  98.0 33.1 %all-to-all-start.3 = ((f32[16,24,128]{2,1,0:T(8,128)}), f32[16,24,128]{2,1,0:T(8,128)S(1)}, u32[]{:S(2)}, u32[]{:S(2)}) async-start(f32[16,24,128]{2,1,0:T(8,128)} %broadcast_in_dim.5), calls=%async_computation.3 | async-start | bytes 393216 | tf_op jit(solution)/shard_map/all_to_all | solution.py:368
  101.6 25.3 %collective-permute-start.6 = (bf16[8,64,128]{2,1,0:T(8,128)(2,1)S(1)}, bf16[8,64,128]{2,1,0:T(8,128)(2,1)S(1)}, u32[]{:S(2)}, u32[]{:S(2)}) collective-permute-start(bf16[8,64,128]{2,1,0:T(8,128)(2,1)S(1)} %copy-done.6), channel_id=1, source_target_pairs={{16,64},{17,65},{18,66},{19,67},{20,68},{21,69},{22,70},{23,71},{2... | collective-permute-start | bytes 393224 | tf_op jit(solution)/shard_map/ppermute | solution.py:457
  106.0 20.9 %collective-permute-start.7 = (bf16[8,64,128]{2,1,0:T(8,128)(2,1)S(1)}, bf16[8,64,128]{2,1,0:T(8,128)(2,1)S(1)}, u32[]{:S(2)}, u32[]{:S(2)}) collective-permute-start(bf16[8,64,128]{2,1,0:T(8,128)(2,1)S(1)} %copy-done.5), channel_id=1, source_target_pairs={{32,64},{33,65},{34,66},{35,67},{36,68},{37,69},{38,70},{39,71},{4... | collective-permute-start | bytes 393224 | tf_op jit(solution)/shard_map/ppermute | solution.py:457
  109.8 17.1 %collective-permute-start.8 = (bf16[8,64,128]{2,1,0:T(8,128)(2,1)S(1)}, bf16[8,64,128]{2,1,0:T(8,128)(2,1)S(1)}, u32[]{:S(2)}, u32[]{:S(2)}) collective-permute-start(bf16[8,64,128]{2,1,0:T(8,128)(2,1)S(1)} %copy-done.4), channel_id=1, source_target_pairs={{48,64},{49,65},{50,66},{51,67},{52,68},{53,69},{54,70},{55,71},{5... | collective-permute-start | bytes 393224 | tf_op jit(solution)/shard_map/ppermute | solution.py:457
  113.5 13.4 %collective-permute-start.9 = (bf16[64,512]{1,0:T(8,128)(2,1)S(1)}, bf16[64,512]{1,0:T(8,128)(2,1)S(1)}, u32[]{:S(2)}, u32[]{:S(2)}) collective-permute-start(bf16[64,512]{1,0:T(8,128)(2,1)S(1)} %copy-done.9), channel_id=1, source_target_pairs={{0,1},{1,2},{2,3},{3,4},{4,5},{5,6},{6,7},{7,8},{8,9},{9,10},{10,1... | collective-permute-start | bytes 196616 | tf_op jit(solution)/shard_map/ppermute | solution.py:439
